TPU v7x, 256 devices: a whole 4x4x8 slice. The times are simulated.
256 devices in a mesh: leaf: 64 (over x, z, core), front: 4 (over y).
Axes of the slice: x: 4, y: 4, z: 8, core: 2. Of those that a mesh axis runs over, the one named last changes fastest.
Arguments:
- child_update: bfloat16 [64, 4, 1, 3, 256, 3072], P('leaf', 'front'), may hold values from -60 to 60, as said below
- sep_one: bfloat16 [64, 4, 1, 4, 256, 512], P('leaf', 'front'), may hold values from -60 to 60, as said below
- sep_two: bfloat16 [64, 4, 1, 4, 256, 256], P('leaf', 'front'), may hold values from -60 to 60, as said below
- map_one: int32 [64, 1, 4, 3], replicated, may hold values from 0 to 3, as said below
- map_two: int32 [32, 1, 4, 3], replicated, may hold values from 0 to 3, as said below
- mask_one: int32 [32, 1, 12, 4], replicated, may hold values 0 or 1
- mask_two: int32 [16, 1, 12, 4], replicated, may hold values 0 or 1
Outputs:
- factor_one: float32 [64, 4, 1, 4, 256, 512], P('leaf', 'front')
- factor_two: float32 [64, 4, 1, 4, 256, 256], P('leaf', 'front')
- update_two: bfloat16 [64, 4, 1, 3, 256, 768], P('leaf', 'front')
Inputs may be any that keep to these rules, and one draw needn't show every extreme that they name: `child_update`: every child[l,b] is symmetric positive definite. `sep_one`: the top 1024 rows of each front's initial entries form a symmetric positive definite block, and every assembled front is positive definite. `sep_two`: the top 1024 rows of each front's initial entries form a symmetric positive definite block, and every assembled front is positive definite. `map_one`: for each child, batch and j the 3 entries are distinct; the two children 2p and 2p + 1 leave out different slots, so every parent tile receives one or two child tiles. `map_two`: for each first-level front, batch and j the 3 entries are distinct; fronts 2q and 2q + 1 leave out different slots, so every parent tile receives one or two child tiles.
All inputs are finite; a program needn't handle non-finite values.
Results may differ from a plain program's by a relative error of at most 0.0047.
Values may be sent and summed in bfloat16 or wider, within the bound.
A program may use at most 192 MiB of HBM per device.

v0:
```python
import jax
import jax.numpy as jnp
from jax import lax
from jax.sharding import PartitionSpec as P

TILE = 256
ST = 4
UT = 12
FT = 16
S = 1024
U = 3072
F = 4096


def swapped(value, axis, apart):
    mask = 2**apart
    pairs = [(source, source ^ mask) for source in range(lax.axis_size(axis))]
    return lax.ppermute(value, axis, pairs)


def place_tiles(blocks, row_source, row_live, col_source, col_live):
    taken = jnp.take(blocks, row_source, axis=0)
    taken = jnp.take(taken, col_source, axis=2)
    keep = jnp.logical_and(row_live[:, None, None, None], col_live[None, None, :, None])
    return jnp.where(keep, taken.astype(jnp.float32), 0.0)


def place_child(child_rows, tile_map, column):
    batch_count = child_rows.shape[0]
    local_tiles = child_rows.shape[1]
    groups = tile_map.shape[1]
    slot_count = FT // groups
    own_slots = lax.dynamic_index_in_dim(tile_map, column, 1, keepdims=False)
    row_hit = own_slots[..., None] == jnp.arange(slot_count, dtype=jnp.int32)
    row_source = jnp.sum(
        row_hit.astype(jnp.int32) * jnp.arange(local_tiles, dtype=jnp.int32)[None, :, None], axis=1
    )
    row_live = jnp.any(row_hit, axis=1)
    targets = (jnp.swapaxes(tile_map, 1, 2) * groups + jnp.arange(groups, dtype=jnp.int32)).reshape(
        batch_count, UT
    )
    col_hit = targets[..., None] == jnp.arange(FT, dtype=jnp.int32)
    col_source = jnp.sum(
        col_hit.astype(jnp.int32) * jnp.arange(UT, dtype=jnp.int32)[None, :, None], axis=1
    )
    col_live = jnp.any(col_hit, axis=1)
    blocks = child_rows.reshape(batch_count, local_tiles, TILE, UT, TILE)
    placed = jax.vmap(place_tiles)(blocks, row_source, row_live, col_source, col_live)
    return placed.reshape(batch_count, slot_count, TILE, F)


def join_halves(mine, other, position):
    lower_first = jnp.concatenate([mine, other], axis=-1)
    upper_first = jnp.concatenate([other, mine], axis=-1)
    return jnp.where(position == 0, lower_first, upper_first)


def add_initial(canvas, initial, mask_front, column):
    batch_count = canvas.shape[0]
    slot_count = canvas.shape[1]
    groups = lax.axis_size("front")
    mask_rows = mask_front.reshape(batch_count, slot_count - 1, groups, ST)
    mask_rows = lax.dynamic_index_in_dim(mask_rows, column, 2, keepdims=False).astype(jnp.float32)
    mask_all = jnp.concatenate([jnp.ones((batch_count, 1, ST), jnp.float32), mask_rows], axis=1)
    weighted = initial.astype(jnp.float32).reshape(batch_count, slot_count, TILE, ST, TILE)
    weighted = (weighted * mask_all[:, :, None, :, None]).reshape(batch_count, slot_count, TILE, S)
    return jnp.concatenate([canvas[:, :, :, :S] + weighted, canvas[:, :, :, S:]], axis=-1)


def factor_front(canvas, column):
    batch_count = canvas.shape[0]
    local_tiles = canvas.shape[1] - 1
    groups = lax.axis_size("front")
    pivot_piece = canvas[:, :1, :, :S]
    pivot_all = lax.all_gather(pivot_piece[None], "front", axis=0, tiled=True)
    pivot_block = jnp.moveaxis(pivot_all, 0, 2).reshape(batch_count, S, S)
    lower_factor = jnp.linalg.cholesky(pivot_block)
    coupling = canvas[:, 1:, :, :S].reshape(batch_count, local_tiles * TILE, S)
    panel_full = lax.linalg.triangular_solve(
        lower_factor, coupling, left_side=False, lower=True, transpose_a=True
    )
    panel_round = panel_full.astype(jnp.bfloat16)
    shared = lax.all_gather(
        panel_round.reshape(batch_count, local_tiles, TILE, S)[None], "front", axis=0, tiled=True
    )
    ordered = jnp.transpose(shared, (1, 2, 0, 3, 4)).reshape(batch_count, U, S)
    own_lower = lax.dynamic_index_in_dim(
        lower_factor.reshape(batch_count, groups, TILE, S), column, 1, keepdims=True
    )
    factor_rows = jnp.concatenate(
        [own_lower, panel_full.reshape(batch_count, local_tiles, TILE, S)], axis=1
    )
    trailing = canvas[:, 1:, :, S:].reshape(batch_count, local_tiles * TILE, U)
    product = jnp.einsum("brk,bnk->brn", panel_round, ordered, preferred_element_type=jnp.float32)
    update = (trailing - product).astype(jnp.bfloat16)
    return (factor_rows, update)


def body(child_update, sep_one, sep_two, map_one, map_two, mask_one, mask_two):
    column = lax.axis_index("front")
    leaf_index = lax.axis_index("leaf")
    half_index = leaf_index % 2
    quarter_index = leaf_index % 4
    pair_index = leaf_index // 2
    quad_index = leaf_index // 4
    side_index = pair_index % 2
    child_rows = child_update[0, 0]
    batch_count = child_rows.shape[0]
    local_tiles = child_rows.shape[1]
    entries_one = sep_one[0, 0]
    entries_two = sep_two[0, 0]
    peer_rows, peer_one, peer_two = swapped((child_rows, entries_one, entries_two), "leaf", 0)
    map_own = lax.dynamic_index_in_dim(map_one, leaf_index, 0, keepdims=False)
    map_peer = lax.dynamic_index_in_dim(map_one, jnp.bitwise_xor(leaf_index, 1), 0, keepdims=False)
    front_first = place_child(child_rows, map_own, column) + place_child(
        peer_rows, map_peer, column
    )
    initial_one = join_halves(entries_one, peer_one, half_index)
    mask_front = lax.dynamic_index_in_dim(mask_one, pair_index, 0, keepdims=False)
    front_first = add_initial(front_first, initial_one, mask_front, column)
    factor_rows_one, update_one = factor_front(front_first, column)
    factor_one = lax.dynamic_slice_in_dim(factor_rows_one, half_index * (S // 2), S // 2, 3)
    entries_half = join_halves(entries_two, peer_two, quarter_index % 2)
    update_far, entries_far = swapped((update_one, entries_half), "leaf", 1)
    map_near = lax.dynamic_index_in_dim(map_two, pair_index, 0, keepdims=False)
    map_far = lax.dynamic_index_in_dim(map_two, jnp.bitwise_xor(pair_index, 1), 0, keepdims=False)
    near_rows = update_one.reshape(batch_count, local_tiles, TILE, U)
    far_rows = update_far.reshape(batch_count, local_tiles, TILE, U)
    front_second = place_child(near_rows, map_near, column) + place_child(far_rows, map_far, column)
    initial_two = join_halves(entries_half, entries_far, side_index)
    mask_second = lax.dynamic_index_in_dim(mask_two, quad_index, 0, keepdims=False)
    front_second = add_initial(front_second, initial_two, mask_second, column)
    factor_rows_two, update_last = factor_front(front_second, column)
    update_last = lax.dynamic_slice_in_dim(update_last, quarter_index * (U // 4), U // 4, 2)
    factor_two = lax.dynamic_slice_in_dim(factor_rows_two, quarter_index * (S // 4), S // 4, 3)
    update_two = update_last.reshape(batch_count, local_tiles, TILE, U // 4)
    return (factor_one[None, None], factor_two[None, None], update_two[None, None])


def solution(mesh):
    return jax.shard_map(
        body,
        mesh=mesh,
        in_specs=(
            P("leaf", "front", None, None, None, None),
            P("leaf", "front", None, None, None, None),
            P("leaf", "front", None, None, None, None),
            P(),
            P(),
            P(),
            P(),
        ),
        out_specs=(
            P("leaf", "front", None, None, None, None),
            P("leaf", "front", None, None, None, None),
            P("leaf", "front", None, None, None, None),
        ),
        check_vma=False,
    )
```

profile of v0, /device:TPU:1, one launch (start us, length us, event | category | flops | bytes accessed | tf_op | source)
XLA Modules:
  0.0 1299.6 jit_solution(7646188197757473696)
XLA Ops:
  74.5 13.8 %select_add_fusion.1 = f32[1,4,256,16,256]{4,2,1,3,0:T(8,128)} fusion(bf16[16,4,256,256]{3,2,1,0:T(8,128)(2,1)} %gather_fusion.3, bf16[16,4,256,256]{3,2,1,0:T(8,128)(2,1)} %gather_fusion.1, pred[16]{0:T(512)(128)(4,1)S(1)} %and_bitcast_fusion.4, pred[16]{0:T(512)(128)(4,1)S(1)} %and_bitcast_fusion.6, pred[4,16]{0,1:T(8,128)(4,1)S(1)} %broadcast_and_fusion.2, ...), kind=kLoop, calls=%fused_computation.13 | loop fusion | flops 29360128 | bytes 33554592 | tf_op jit(solution)/shard_map/add | solution.py:115
  88.3 16.4 %copy.145 = f32[1,4,256,16,256]{2,4,3,1,0:T(8,128)} copy(f32[1,4,256,16,256]{4,2,1,3,0:T(8,128)} %select_add_fusion.1) | data formatting | bytes 33554432 | tf_op jit(solution)/shard_map/add | solution.py:115
  116.7 47.7 %all-gather.11.cloned.1.call-done = f32[4,1,256,1024]{3,2,1,0:T(8,128)} async-done(((f32[1,1,256,1024]{3,2,1,0:T(8,128)}), f32[4,1,256,1024]{3,2,1,0:T(8,128)}) %all-gather.11.cloned.1.call-update) | async-done | bytes 4194320 | tf_op jit(solution)/shard_map/all_gather | solution.py:75
  176.3 11.7 custom-call.91
  204.9 11.9 custom-call.93
  231.2 11.7 custom-call.95
  257.6 12.1 custom-call.97
  284.3 11.7 custom-call.99
  297.4 9.9 custom-call.100
  310.7 11.7 custom-call.101
  336.5 11.9 custom-call.103
  362.1 11.7 custom-call.105
  387.6 28.1 %while.4 = (s32[]{:T(128)}, f32[1,1024,1024]{2,1,0:T(8,128)}, s32[8,2]{0,1:T(2,128)S(1)}, f32[8,1,128,128]{3,2,1,0:T(8,128)}, s32[]{:T(128)}) while((s32[]{:T(128)}, f32[1,1024,1024]{2,1,0:T(8,128)}, s32[8,2]{0,1:T(2,128)S(1)}, f32[8,1,128,128]{3,2,1,0:T(8,128)}, s32[]{:T(128)}) %tuple.131), condition=%wide.while_cond, body=%wide.while_body.sunk | while | flops 2 | bytes 132205 | solution.py:79
  415.7 80.5 %custom-call.106 = f32[1,8,128,128]{2,3,1,0:T(8,128)} custom-call(f32[1,8,128,128]{3,2,1,0:T(8,128)} %bitcast.928), custom_call_target="InvertDiagBlocksLowerTriangular" | custom-call | tf_op jit(solution)/shard_map/triangular_solve/custom-call.7 | solution.py:79
  549.4 50.9 %all-gather.7.cloned.1.call-done = bf16[4,1,3,256,1024]{4,3,2,1,0:T(8,128)(2,1)} async-done(((bf16[1,1,3,256,1024]{4,3,2,1,0:T(8,128)(2,1)}), bf16[4,1,3,256,1024]{4,3,2,1,0:T(8,128)(2,1)}) %all-gather.7.cloned.1.call-update) | async-done | bytes 6291472 | tf_op jit(solution)/shard_map/all_gather | solution.py:83
  654.5 62.0 %collective-permute-done.2 = bf16[1,768,3072]{2,1,0:T(8,128)(2,1)} collective-permute-done((bf16[1,768,3072]{2,1,0:T(8,128)(2,1)}, bf16[1,768,3072]{2,1,0:T(8,128)(2,1)}, u32[]{:S(2)}, u32[]{:S(2)}) %collective-permute-start.2) | collective-permute-done | bytes 4718624 | tf_op jit(solution)/shard_map/ppermute | solution.py:18
  752.0 13.8 %select_add_fusion = f32[1,4,256,16,256]{4,2,1,3,0:T(8,128)} fusion(bf16[16,4,256,256]{3,2,1,0:T(8,128)(2,1)} %gather_fusion.7, bf16[16,4,256,256]{3,2,1,0:T(8,128)(2,1)} %gather_fusion.5, pred[16]{0:T(512)(128)(4,1)S(1)} %and_bitcast_fusion, pred[16]{0:T(512)(128)(4,1)S(1)} %and_bitcast_fusion.2, pred[4,16]{0,1:T(8,128)(4,1)S(1)} %broadcast_and_fusion, ...), kind=kLoop, calls=%fused_computation.12 | loop fusion | flops 29360128 | bytes 33554592 | tf_op jit(solution)/shard_map/add | solution.py:129
  765.8 16.4 %copy.163 = f32[1,4,256,16,256]{2,4,3,1,0:T(8,128)} copy(f32[1,4,256,16,256]{4,2,1,3,0:T(8,128)} %select_add_fusion) | data formatting | bytes 33554432 | tf_op jit(solution)/shard_map/add | solution.py:129
  793.4 49.4 %all-gather.13.cloned.1.call-done = f32[4,1,256,1024]{3,2,1,0:T(8,128)} async-done(((f32[1,1,256,1024]{3,2,1,0:T(8,128)}), f32[4,1,256,1024]{3,2,1,0:T(8,128)}) %all-gather.13.cloned.1.call-update) | async-done | bytes 4194320 | tf_op jit(solution)/shard_map/all_gather | solution.py:75
  854.7 11.7 custom-call.111
  883.4 11.9 custom-call.113
  909.7 11.7 custom-call.115
  936.1 12.1 custom-call.117
  962.8 11.7 custom-call.119
  975.8 9.9 custom-call.120
  989.1 11.7 custom-call.121
  1014.8 11.9 custom-call.123
  1040.5 11.7 custom-call.125
  1066.1 28.1 %while.5 = (s32[]{:T(128)}, f32[1,1024,1024]{2,1,0:T(8,128)}, s32[8,2]{0,1:T(2,128)S(1)}, f32[8,1,128,128]{3,2,1,0:T(8,128)}, s32[]{:T(128)}) while((s32[]{:T(128)}, f32[1,1024,1024]{2,1,0:T(8,128)}, s32[8,2]{0,1:T(2,128)S(1)}, f32[8,1,128,128]{3,2,1,0:T(8,128)}, s32[]{:T(128)}) %tuple.145), condition=%wide.while_cond.clone, body=%wide.while_body.clone.sunk | while | flops 2 | bytes 132205 | solution.py:79
  1094.2 80.4 %custom-call.126 = f32[1,8,128,128]{2,3,1,0:T(8,128)} custom-call(f32[1,8,128,128]{3,2,1,0:T(8,128)} %bitcast.927), custom_call_target="InvertDiagBlocksLowerTriangular" | custom-call | tf_op jit(solution)/shard_map/triangular_solve/custom-call.7 | solution.py:79
  1227.8 10.1 copy.173
  1243.9 37.3 %all-gather.9.cloned.1.call-done = bf16[4,1,3,256,1024]{4,3,2,1,0:T(8,128)(2,1)} async-done(((bf16[1,1,3,256,1024]{4,3,2,1,0:T(8,128)(2,1)}), bf16[4,1,3,256,1024]{4,3,2,1,0:T(8,128)(2,1)}) %all-gather.9.cloned.1.call-update) | async-done | bytes 6291472 | tf_op jit(solution)/shard_map/all_gather | solution.py:83
  (354 shorter events, 587.2 us)
Async XLA Ops:
  7.2 11.9 copy-start
  7.2 157.2 %all-gather.11.cloned.1.call-start = ((), (), s32[]{:S(2)}) async-start(), calls=%async_computation.2 | async-start | bytes 5242880 | tf_op jit(solution)/shard_map/all_gather | solution.py:75
  8.7 10.0 copy-start.18
  8.7 10.8 copy-start.19
  8.7 11.2 copy-start.17
  8.7 95.9 %collective-permute-start.1 = (bf16[1,4,256,512]{2,3,1,0:T(8,128)(2,1)S(1)}, bf16[1,4,256,512]{2,3,1,0:T(8,128)(2,1)S(1)}, u32[]{:S(2)}, u32[]{:S(2)}) collective-permute-start(bf16[1,4,256,512]{2,3,1,0:T(8,128)(2,1)S(1)} %bitcast.921), channel_id=1, source_target_pairs={{0,4},{4,0},{8,12},{12,8},{16,20},{20,16},{24,28},{28,24},{32,36},... | collective-permute-start | bytes 3145736 | tf_op jit(solution)/shard_map/ppermute | solution.py:18
  18.7 29.6 %collective-permute-start = (bf16[1,3,256,3072]{2,3,1,0:T(8,128)(2,1)}, bf16[1,3,256,3072]{2,3,1,0:T(8,128)(2,1)}, u32[]{:S(2)}, u32[]{:S(2)}) collective-permute-start(bf16[1,3,256,3072]{2,3,1,0:T(8,128)(2,1)} %bitcast.880), channel_id=1, source_target_pairs={{0,4},{4,0},{8,12},{12,8},{16,20},{20,16},{24,28},{28,24},{32,36},... | collective-permute-start | bytes 14155784 | tf_op jit(solution)/shard_map/ppermute | solution.py:18
  109.0 2.0 copy-start.2
  112.3 1.9 slice-start
  112.4 488.0 %all-gather.7.cloned.1.call-start = ((), (), s32[]{:S(2)}) async-start(), calls=%async_computation | async-start | bytes 7864320 | tf_op jit(solution)/shard_map/all_gather | solution.py:83
  174.3 1.9 copy-start.10
  380.0 116.2 %copy-start.9 = (f32[1,3,256,1024]{3,2,1,0:T(8,128)S(1)}, f32[1,3,256,1024]{3,2,1,0:T(8,128)}, u32[]{:S(2)}) copy-start(f32[1,3,256,1024]{3,2,1,0:T(8,128)} %copy.152) | copy-start | bytes 9437188
  496.2 6.9 copy-start.14
  528.2 1.7 copy-start.4
  531.6 311.2 %all-gather.13.cloned.1.call-start = ((), (), s32[]{:S(2)}) async-start(), calls=%async_computation.3 | async-start | bytes 5242880 | tf_op jit(solution)/shard_map/all_gather | solution.py:75
  600.4 5.5 copy-start.12
  605.9 8.9 copy-start.16
  613.5 102.9 %collective-permute-start.2 = (bf16[1,768,3072]{2,1,0:T(8,128)(2,1)}, bf16[1,768,3072]{2,1,0:T(8,128)(2,1)}, u32[]{:S(2)}, u32[]{:S(2)}) collective-permute-start(bf16[1,768,3072]{2,1,0:T(8,128)(2,1)} %bitcast.920), channel_id=1, source_target_pairs={{0,8},{4,12},{8,0},{12,4},{16,24},{20,28},{24,16},{28,20},{32,40},... | collective-permute-start | bytes 14155784 | tf_op jit(solution)/shard_map/ppermute | solution.py:18
  615.0 2.6 collective-permute-start.3
  617.9 164.3 %collective-permute-start.4 = (bf16[1,4,256,512]{2,3,1,0:T(8,128)(2,1)S(1)}, bf16[1,4,256,512]{2,3,1,0:T(8,128)(2,1)}, u32[]{:S(2)}, u32[]{:S(2)}) collective-permute-start(bf16[1,4,256,512]{2,3,1,0:T(8,128)(2,1)S(1)} %maximum_select_fusion.3), channel_id=1, source_target_pairs={{0,8},{4,12},{8,0},{12,4},{16,24},{20,28},{24,16},{28,20},{32,40},... | collective-permute-start | bytes 3145736 | tf_op jit(solution)/shard_map/ppermute | solution.py:18
  785.7 2.0 copy-start.3
  789.1 1.9 slice-start.1
  789.1 492.0 %all-gather.9.cloned.1.call-start = ((), (), s32[]{:S(2)}) async-start(), calls=%async_computation.1 | async-start | bytes 7864320 | tf_op jit(solution)/shard_map/all_gather | solution.py:83
  852.8 1.9 copy-start.11
  1058.5 116.1 %copy-start.8 = (f32[1,3,256,1024]{3,2,1,0:T(8,128)S(1)}, f32[1,3,256,1024]{3,2,1,0:T(8,128)}, u32[]{:S(2)}) copy-start(f32[1,3,256,1024]{3,2,1,0:T(8,128)} %copy.171) | copy-start | bytes 9437188
  1174.6 6.9 copy-start.15
  1206.5 1.7 copy-start.6
  1208.3 4.1 copy-start.5
  1227.8 10.1 copy-start.7
  1243.9 40.8 %copy-start.13 = (bf16[1,768,1024]{1,2,0:T(8,128)(2,1)S(1)}, bf16[1,768,1024]{1,2,0:T(8,128)(2,1)}, u32[]{:S(2)}) copy-start(bf16[1,768,1024]{1,2,0:T(8,128)(2,1)} %convert_element_type.105) | copy-start | bytes 4718596
  1284.6 8.2 copy-start.1
Sparse Core Ops, SparseCore 0:
  112.5 51.8 all-gather.10
  531.7 68.5 all-gather.6
  789.2 53.5 all-gather.12
  1212.5 68.5 all-gather.8
where the time goes:
time: 1310 us; the launch traced here: 1300 us
  other arithmetic  602 us (46%)
  local copies, waits for them, and re-layouts  296 us (23%)
  waiting for transfers between devices  248 us (19%)
  matrix products  123 us (9%)
  between operations  25 us (2%)
    another operation x62, other arithmetic, factor_front(): lower_factor = jnp.linalg.cholesky(pivot_block)  346 us
    another operation x5, other arithmetic, factor_front(): lax.linalg.triangular_solve(lower_factor, coupling, left_side=False, lowe...  174 us
    all_gather x2, waiting for transfers between devices, factor_front(): pivot_all = lax.all_gather(pivot_piece[None], 'front', axis=0, tiled=True)  97.2 us
    all_gather x2, waiting for transfers between devices, factor_front(): lax.all_gather(panel_round.reshape(batch_count, local_tiles, TILE, S)[Non...  88.2 us
    another operation x30, matrix products, factor_front(): lax.linalg.triangular_solve(lower_factor, coupling, left_side=False, lowe...  63.6 us
    another operation x53, local copies, waits for them, and re-layouts, factor_front(): lax.linalg.triangular_solve(lower_factor, coupling, left_side=False, lowe...  62.7 us
    ppermute x5, waiting for transfers between devices, swapped(): return lax.ppermute(value, axis, pairs)  62.4 us
    another operation x28, matrix products, factor_front(): lower_factor = jnp.linalg.cholesky(pivot_block)  46.3 us
  transfers between devices with their start and end apart: 9, of which 6 were waited for; matrix products, arithmetic and copies ran while one was open for 19% of the time, Pallas kernels for 0%

commit v1 on v0

v1 whole, which is shorter than its diff:
```python
import functools

import jax
import jax.numpy as jnp
from jax import lax
from jax.experimental import pallas as pl
from jax.experimental.pallas import tpu as pltpu
from jax.sharding import PartitionSpec as P

TILE = 256
ST = 4
UT = 12
S = 1024
U = 3072
C = 768
G = 128
F32 = jnp.float32
BF16 = jnp.bfloat16
VMEM_LIMIT = 60 * 1024 * 1024


def swapped(value, axis, apart):
    mask = 2**apart
    pairs = [(source, source ^ mask) for source in range(lax.axis_size(axis))]
    return lax.ppermute(value, axis, pairs)


def dot_nt(x, y):
    return lax.dot_general(x, y, (((1,), (1,)), ((), ())), preferred_element_type=F32)


def split(x):
    high = x.astype(BF16)
    return high, (x - high.astype(F32)).astype(BF16)


def left_parts(x):
    high, low = split(x)
    return jnp.concatenate([high, low, high], axis=1)


def right_parts(x):
    high, low = split(x)
    return jnp.concatenate([high, high, low], axis=1)


def source_of(map_ref, base, group, slot):
    first = map_ref[base + group * 3] == slot
    second = map_ref[base + group * 3 + 1] == slot
    third = map_ref[base + group * 3 + 2] == slot
    index = jnp.where(first, 0, jnp.where(second, 1, 2))
    live = jnp.logical_or(first, jnp.logical_or(second, third))
    return index, live


def invert_diagonal(block_ref, inverse_ref):
    sub = lax.broadcasted_iota(jnp.int32, (8, G), 0)
    lane = lax.broadcasted_iota(jnp.int32, (8, G), 1)
    slabs = G // 8
    rest = [block_ref[8 * r : 8 * r + 8, :] for r in range(slabs)]
    unit = [jnp.where(lane == sub + 8 * r, 1.0, 0.0).astype(F32) for r in range(slabs)]

    def lanes(v, c):
        return jnp.broadcast_to(v[:, c : c + 1], (8, G))

    def rows(v, i):
        return jnp.broadcast_to(v[i : i + 1, :], (8, G))

    for t in range(slabs):
        k = 8 * t
        cols = [lanes(rest[t], k + i) for i in range(8)]
        a = {(i, j): rows(cols[j], i) for j in range(8) for i in range(j, 8)}
        low = {}
        scale = []
        for i in range(8):
            scale.append(lax.rsqrt(a[i, i]))
            for j in range(i + 1, 8):
                low[j, i] = a[j, i] * scale[i]
            for j in range(i + 1, 8):
                for m in range(j, 8):
                    a[m, j] = a[m, j] - low[m, i] * low[j, i]

        def forward(pick):
            out = []
            for i in range(8):
                x = pick(i)
                for j in range(i):
                    x = x - low[i, j] * out[j]
                out.append(x * scale[i])
            return out

        upper = forward(lambda i: rows(rest[t], i))
        inv = forward(lambda i: rows(unit[t], i))
        packed = inv[0]
        for i in range(1, 8):
            packed = jnp.where(sub == i, inv[i], packed)
        inverse_ref[k : k + 8, :] = packed
        for r in range(t + 1, slabs):
            column = []
            for i in range(8):
                x = lanes(rest[r], k + i)
                for j in range(i):
                    x = x - column[j] * low[i, j]
                column.append(x * scale[i])
            for i in range(8):
                rest[r] = rest[r] - column[i] * upper[i]
                unit[r] = unit[r] - column[i] * inv[i]


def positions(level):
    leaf = lax.axis_index("leaf")
    group = lax.axis_index("front")
    child = leaf if level == 1 else leaf // 2
    half = child % 2
    return leaf, group, child, half


def initial_tile(own_ref, peer_ref, m, c, half):
    at = (m, slice(None), slice((c % 2) * TILE, (c % 2 + 1) * TILE))
    return jnp.where(half == c // 2, own_ref[at].astype(F32), peer_ref[at].astype(F32))


def pivot_kernel(level, map_ref, own_ref, peer_ref, init_own, init_peer, out_ref, tiles, sems):
    leaf, group, child, half = positions(level)
    places = []
    for side, ref in ((0, own_ref), (1, peer_ref)):
        base = (child ^ side) * 12
        row, row_live = source_of(map_ref, base, group, 0)
        for c in range(ST):
            col, col_live = source_of(map_ref, base, c, 0)
            start = pl.multiple_of((col * 4 + c) * TILE, TILE)
            copy = pltpu.make_async_copy(
                ref.at[row, :, pl.ds(start, TILE)], tiles.at[side, c], sems.at[side, c]
            )
            copy.start()
            places.append((copy, jnp.logical_and(row_live, col_live)))
    for copy, _ in places:
        copy.wait()
    for c in range(ST):
        own = jnp.where(places[c][1], tiles[0, c].astype(F32), 0.0)
        peer = jnp.where(places[ST + c][1], tiles[1, c].astype(F32), 0.0)
        init = initial_tile(init_own, init_peer, 0, c, half)
        out_ref[:, c * TILE : (c + 1) * TILE] = own + peer + init


def pivot_rows(level, tile_map, own, peer, init_own, init_peer):
    init_spec = pl.BlockSpec(memory_space=pltpu.VMEM)
    return pl.pallas_call(
        functools.partial(pivot_kernel, level),
        out_shape=jax.ShapeDtypeStruct((TILE, S), F32),
        in_specs=[
            pl.BlockSpec(memory_space=pltpu.SMEM),
            pl.BlockSpec(memory_space=pl.ANY),
            pl.BlockSpec(memory_space=pl.ANY),
            init_spec,
            init_spec,
        ],
        scratch_shapes=[
            pltpu.VMEM((2, ST, TILE, TILE), BF16),
            pltpu.SemaphoreType.DMA((2, ST)),
        ],
        name=f"pivot_{level}",
    )(tile_map, own, peer, init_own, init_peer)


def factor_kernel(
    level, map_ref, mask_ref, pivot_ref, own_ref, peer_ref, init_own, init_peer,
    factor_ref, panel_ref, a_ref, l_ref, xl_ref, xr_ref, inv_ref, tiles, sems
):
    leaf, group, child, half = positions(level)
    width = S // (2 * level)
    copies = []
    lives = {}
    for side, ref in ((0, own_ref), (1, peer_ref)):
        base = (child ^ side) * 12
        for m in range(1, 4):
            row, row_live = source_of(map_ref, base, group, m)
            for c in range(ST):
                col, col_live = source_of(map_ref, base, c, 0)
                start = pl.multiple_of((col * 4 + c) * TILE, TILE)
                slot = (m - 1) * ST + c
                copy = pltpu.make_async_copy(
                    ref.at[row, :, pl.ds(start, TILE)], tiles.at[side, slot], sems.at[side, slot]
                )
                copy.start()
                copies.append(copy)
                lives[side, slot] = jnp.logical_and(row_live, col_live)
    for t in range(ST):
        a_ref[t * TILE : (t + 1) * TILE, :] = pivot_ref[t]
    for copy in copies:
        copy.wait()
    for m in range(1, 4):
        for c in range(ST):
            slot = (m - 1) * ST + c
            own = jnp.where(lives[0, slot], tiles[0, slot].astype(F32), 0.0)
            peer = jnp.where(lives[1, slot], tiles[1, slot].astype(F32), 0.0)
            keep = mask_ref[((child // 2) * UT + (m - 1) * 4 + group) * ST + c].astype(F32)
            init = initial_tile(init_own, init_peer, m, c, half) * keep
            a_ref[S + (m - 1) * TILE : S + m * TILE, c * TILE : (c + 1) * TILE] = own + peer + init

    def step(g, _):
        cols = pl.ds(pl.multiple_of(g * G, G), G)
        invert_diagonal(a_ref.at[cols, cols], inv_ref)
        inverse = right_parts(inv_ref[...])

        def panel(low, high):
            x = dot_nt(left_parts(a_ref[low:high, cols]), inverse)
            l_ref[low:high, cols] = x
            xl_ref[low:high, :] = left_parts(x)
            if low < S:
                xr_ref[low:high, :] = right_parts(x)

        @pl.when(g < 4)
        def _():
            panel(0, S // 2)

        panel(S // 2, S)
        panel(S, S + C)
        for block in range(ST):

            @pl.when(g < 2 * block + 1)
            def _():
                there = slice(block * TILE, (block + 1) * TILE)
                a_ref[block * TILE :, there] -= dot_nt(xl_ref[block * TILE :, :], xr_ref[there, :])

        return 0

    lax.fori_loop(0, S // G, step, 0)
    part = pl.ds(pl.multiple_of((leaf % (2 * level)) * width, width), width)
    row = lax.broadcasted_iota(jnp.int32, (TILE, width), 0) + group * TILE
    col = lax.broadcasted_iota(jnp.int32, (TILE, width), 1) + (leaf % (2 * level)) * width
    own_rows = l_ref[pl.ds(pl.multiple_of(group * TILE, TILE), TILE), part]
    factor_ref[0] = jnp.where(row >= col, own_rows, 0.0)
    for m in range(1, 4):
        factor_ref[m] = l_ref[S + (m - 1) * TILE : S + m * TILE, part]
    panel_ref[...] = l_ref[S:, :].astype(BF16)


def factor_rows(level, tile_map, tile_mask, pivot, own, peer, init_own, init_peer):
    width = S // (2 * level)
    vmem = pl.BlockSpec(memory_space=pltpu.VMEM)
    smem = pl.BlockSpec(memory_space=pltpu.SMEM)
    hbm = pl.BlockSpec(memory_space=pl.ANY)
    return pl.pallas_call(
        functools.partial(factor_kernel, level),
        out_shape=[
            jax.ShapeDtypeStruct((4, TILE, width), F32),
            jax.ShapeDtypeStruct((C, S), BF16),
        ],
        in_specs=[smem, smem, vmem, hbm, hbm, vmem, vmem],
        scratch_shapes=[
            pltpu.VMEM((S + C, S), F32),
            pltpu.VMEM((S + C, S), F32),
            pltpu.VMEM((S + C, 3 * G), BF16),
            pltpu.VMEM((S, 3 * G), BF16),
            pltpu.VMEM((G, G), F32),
            pltpu.VMEM((2, 12, TILE, TILE), BF16),
            pltpu.SemaphoreType.DMA((2, 12)),
        ],
        compiler_params=pltpu.CompilerParams(vmem_limit_bytes=VMEM_LIMIT),
        name=f"factor_{level}",
    )(tile_map, tile_mask, pivot, own, peer, init_own, init_peer)


def update_kernel(level, map_ref, x_ref, y_ref, *rest):
    tiles, out_ref = rest[:6], rest[6]
    leaf, group, child, half = positions(level)
    v = pl.program_id(0) + (0 if level == 1 else (leaf % 4) * 3)
    product = dot_nt(x_ref[...], y_ref[0])
    for m in range(1, 4):
        total = -product[(m - 1) * TILE : m * TILE, :]
        for side in (0, 1):
            base = (child ^ side) * 12
            _, row_live = source_of(map_ref, base, group, m)
            _, col_live = source_of(map_ref, base, v % 4, 1 + v // 4)
            live = jnp.logical_and(row_live, col_live)
            total = total + jnp.where(live, tiles[2 * (m - 1) + side][0].astype(F32), 0.0)
        out_ref[m - 1] = total.astype(BF16)


def update_rows(level, tile_map, panel, panels, own, peer):
    def offset():
        return 0 if level == 1 else (lax.axis_index("leaf") % 4) * 3

    place = jnp.stack([lax.axis_index("leaf"), lax.axis_index("front")]).astype(jnp.int32)

    def start(v, place_ref):
        return v + (0 if level == 1 else (place_ref[0] % 4) * 3)

    def panel_block(v, place_ref, map_ref):
        at = start(v, place_ref)
        return (at % 4, at // 4, 0)

    def tile_block(m, side, v, place_ref, map_ref):
        at = start(v, place_ref)
        child = place_ref[0] if level == 1 else place_ref[0] // 2
        base = (child ^ side) * 12
        row, _ = source_of(map_ref, base, place_ref[1], m)
        col, _ = source_of(map_ref, base, at % 4, 1 + at // 4)
        return (row, 0, col * 4 + at % 4)

    def kernel(place_ref, map_ref, *refs):
        update_kernel(level, map_ref, *refs)

    count = 12 if level == 1 else 3
    tile_specs = [
        pl.BlockSpec((1, TILE, TILE), functools.partial(tile_block, m, side))
        for m in range(1, 4)
        for side in (0, 1)
    ]
    return pl.pallas_call(
        kernel,
        out_shape=jax.ShapeDtypeStruct((3, TILE, TILE * count), BF16),
        grid_spec=pltpu.PrefetchScalarGridSpec(
            num_scalar_prefetch=2,
            grid=(count,),
            in_specs=[
                pl.BlockSpec((C, S), lambda v, p, q: (0, 0)),
                pl.BlockSpec((1, TILE, S), panel_block),
                *tile_specs,
            ],
            out_specs=pl.BlockSpec((3, TILE, TILE), lambda v, p, q: (0, 0, v)),
        ),
        compiler_params=pltpu.CompilerParams(vmem_limit_bytes=VMEM_LIMIT),
        name=f"update_{level}",
    )(place, tile_map, panel, panels, *([own, peer] * 3))


def join_halves(mine, other, position):
    lower_first = jnp.concatenate([mine, other], axis=-1)
    upper_first = jnp.concatenate([other, mine], axis=-1)
    return jnp.where(position == 0, lower_first, upper_first)


def level_step(level, tile_map, tile_mask, own, peer, init_own, init_peer):
    pivot = pivot_rows(level, tile_map, own, peer, init_own, init_peer)
    pivots = lax.all_gather(pivot, "front", axis=0)
    factor, panel = factor_rows(level, tile_map, tile_mask, pivots, own, peer, init_own, init_peer)
    panels = lax.all_gather(panel, "front", axis=0)
    update = update_rows(level, tile_map, panel, panels, own, peer)
    return factor, update


def body(child_update, sep_one, sep_two, map_one, map_two, mask_one, mask_two):
    leaf = lax.axis_index("leaf")
    own = child_update[0, 0, 0]
    init_own = sep_one[0, 0, 0]
    quarter = sep_two[0, 0, 0]
    peer, init_peer, quarter_peer = swapped((own, init_own, quarter), "leaf", 0)
    factor_one, update_one = level_step(
        1, map_one.reshape(-1), mask_one.reshape(-1), own, peer, init_own, init_peer
    )
    near = join_halves(quarter, quarter_peer, leaf % 2)
    far_update, far = swapped((update_one, near), "leaf", 1)
    factor_two, update_two = level_step(
        2, map_two.reshape(-1), mask_two.reshape(-1), update_one, far_update, near, far
    )
    return (factor_one[None, None, None], factor_two[None, None, None], update_two[None, None, None])


def solution(mesh):
    split_spec = P("leaf", "front", None, None, None, None)
    return jax.shard_map(
        body,
        mesh=mesh,
        in_specs=(split_spec, split_spec, split_spec, P(), P(), P(), P()),
        out_specs=(split_spec, split_spec, split_spec),
        check_vma=False,
    )
```

time: 1310 us -> 533 us (0.41)
  other arithmetic: 602 us -> 0.9 us
  local copies, waits for them, and re-layouts: 296 us -> 5.79 us
  Pallas kernels: 0 us -> 137 us
  matrix products: 123 us -> 0 us
  waiting for transfers between devices: 248 us -> 368 us
    another operation x67 -> x1, other arithmetic: 520 us -> 0.65 us  [update_rows(): jnp.stack([lax.axis_index('leaf'), lax.axis_index('front')])]
    pallas_call x0 -> x6, Pallas kernels: none -> 137 us  [the longest x2 107 us: factor_rows(): pl.pallas_call(functools.partial(factor_kernel, level), out_shape=[jax.Sh...]
    another operation x76 -> x0, local copies, waits for them, and re-layouts: 118 us -> none  [the longest x53 62.7 us: factor_front(): lax.linalg.triangular_solve(lower_factor, coupling, left_side=False, lowe...]
    another operation x58 -> x0, matrix products: 110 us -> none  [the longest x30 63.6 us: factor_front(): lax.linalg.triangular_solve(lower_factor, coupling, left_side=False, lowe...]
    ppermute x5, waiting for transfers between devices: 62.4 us -> 129 us  [swapped(): return lax.ppermute(value, axis, pairs)]
    gather x15 -> x0, local copies, waits for them, and re-layouts: 54.1 us -> none  [the longest x8 30.2 us: place_tiles(): taken = jnp.take(taken, col_source, axis=2)]
    all_gather x4, waiting for transfers between devices: 185 us -> 239 us  [the longest x2 137 us: level_step(): panels = lax.all_gather(panel, 'front', axis=0)]
    slice x14 -> x0, local copies, waits for them, and re-layouts: 47.6 us -> none  [the longest x4 36.4 us: factor_front(): trailing = canvas[:, 1:, :, S:].reshape(batch_count, local_tiles * TILE, U)]
  transfers between devices with their start and end apart: 9 -> 9, of which waited for: 6 -> 8; matrix products, arithmetic and copies ran while one was open for 19% -> 1% of each run, Pallas kernels for 0% -> 0%
where the time goes in v1:
time: 533 us; the launch traced here: 532 us
  waiting for transfers between devices  368 us (69%)
  Pallas kernels  137 us (26%)
  between operations  13.9 us (3%)
  starting transfers between devices  6.12 us (1%)
  local copies, waits for them, and re-layouts  5.79 us (1%)
    all_gather x2, waiting for transfers between devices, level_step(): panels = lax.all_gather(panel, 'front', axis=0)  137 us
    ppermute x5, waiting for transfers between devices, swapped(): return lax.ppermute(value, axis, pairs)  129 us
    pallas_call x2, Pallas kernels, factor_rows(): pl.pallas_call(functools.partial(factor_kernel, level), out_shape=[jax.Sh...  107 us
    all_gather x2, waiting for transfers between devices, level_step(): pivots = lax.all_gather(pivot, 'front', axis=0)  102 us
    pallas_call x2, Pallas kernels, update_rows(): pl.pallas_call(kernel, out_shape=jax.ShapeDtypeStruct((3, TILE, TILE * co...  22.2 us
  transfers between devices with their start and end apart: 9, of which 8 were waited for; matrix products, arithmetic and copies ran while one was open for 1% of the time, Pallas kernels for 0%

profile of v1, /device:TPU:1, one launch (start us, length us, event | category | flops | bytes accessed | tf_op | source)
XLA Modules:
  0.0 532.4 jit_solution(9326631188821824827)
XLA Ops:
  7.2 3.3 collective-permute-start
  10.5 0.1 collective-permute-start.1
  10.6 0.8 copy.10
  11.5 0.8 reshape.18.map_ref
  12.3 7.2 %collective-permute-done.1.init_peer = bf16[4,256,512]{2,1,0:T(8,128)(2,1)S(1)} collective-permute-done((bf16[4,256,512]{2,1,0:T(8,128)(2,1)}, bf16[4,256,512]{2,1,0:T(8,128)(2,1)S(1)}, u32[]{:S(2)}, u32[]{:S(2)}) %collective-permute-start.1) | collective-permute-done | bytes 1048608 | tf_op jit(solution)/shard_map/ppermute | solution.py:25
  19.4 0.5 collective-permute-done.peer_ref.refs_3_.refs_5_.refs_7_
  19.9 0.5 copy-done.1
  20.4 4.2 pivot_1.1
  24.7 0.2 copy.11
  24.9 0.7 reshape.19.mask_ref
  25.6 50.7 %all-gather.9.cloned.1.call-done = f32[1024,1024]{1,0:T(8,128)} async-done(((f32[256,1024]{1,0:T(8,128)}), f32[1024,1024]{1,0:T(8,128)}) %all-gather.9.cloned.1.call-update) | async-done | bytes 4194320 | tf_op jit(solution)/shard_map/all_gather | solution.py:337
  76.4 53.5 %factor_1.1 = (f32[4,256,512]{2,1,0:T(8,128)}, bf16[768,1024]{1,0:T(8,128)(2,1)}) custom-call(s32[768]{0:T(1024)} %reshape.18.map_ref, s32[1536]{0:T(1024)} %reshape.19.mask_ref, f32[4,256,1024]{2,1,0:T(8,128)} %bitcast.32, bf16[3,256,3072]{2,1,0:T(8,128)(2,1)} %bitcast.22, bf16[3,256,3072]{2,1,0:T(8,128)(2,1)} %collective-permute-done.peer_ref.refs_3_.refs_5_.refs_7_, ...), custom_call_target="tpu_custom_call" | custom-call | tf_op jit(solution)/shard_map/factor_1/pallas_call | solution.py:244
  129.9 0.0 all-gather.13.cloned.1.call-start
  130.0 0.7 pad_add_fusion.place_ref
  130.6 68.0 %all-gather.11.cloned.1.call-done = bf16[3072,1024]{1,0:T(8,128)(2,1)} async-done(((bf16[768,1024]{1,0:T(8,128)(2,1)}), bf16[3072,1024]{1,0:T(8,128)(2,1)}) %all-gather.11.cloned.1.call-update) | async-done | bytes 6291472 | tf_op jit(solution)/shard_map/all_gather | solution.py:339
  198.6 15.8 %update_1.1.own_ref.refs_2_.refs_4_.refs_6_ = bf16[3,256,3072]{2,1,0:T(8,128)(2,1)} custom-call(s32[2]{0:T(128)} %pad_add_fusion.place_ref, s32[768]{0:T(1024)} %reshape.18.map_ref, bf16[768,1024]{1,0:T(8,128)(2,1)} %get-tuple-element.8.refs_0_, bf16[4,768,1024]{2,1,0:T(8,128)(2,1)} %bitcast.27, bf16[3,256,3072]{2,1,0:T(8,128)(2,1)} %bitcast.23, ...), custom_call_target="tpu_custom_call" | custom-call | tf_op jit(solution)/shard_map/update_1/pallas_call | solution.py:311
  214.5 1.3 collective-permute-start.2
  215.8 0.9 collective-permute-start.3
  216.7 1.5 collective-permute-done.3
  218.3 0.2 maximum_select_fusion.init_own
  218.5 0.3 collective-permute-start.4
  218.8 0.1 copy.12
  218.9 0.8 reshape.20.map_ref
  219.7 120.1 %collective-permute-done.4.init_peer = bf16[4,256,512]{2,1,0:T(8,128)(2,1)S(1)} collective-permute-done((bf16[4,256,512]{2,1,0:T(8,128)(2,1)S(1)}, bf16[4,256,512]{2,1,0:T(8,128)(2,1)S(1)}, u32[]{:S(2)}, u32[]{:S(2)}) %collective-permute-start.4) | collective-permute-done | bytes 1048608 | tf_op jit(solution)/shard_map/ppermute | solution.py:25
  339.8 1.0 copy-done.2
  340.8 4.2 pivot_2.1
  345.1 0.2 copy.13
  345.3 0.7 reshape.21.mask_ref
  346.0 51.6 %all-gather.13.cloned.1.call-done = f32[1024,1024]{1,0:T(8,128)} async-done(((f32[256,1024]{1,0:T(8,128)}), f32[1024,1024]{1,0:T(8,128)}) %all-gather.13.cloned.1.call-update) | async-done | bytes 4194320 | tf_op jit(solution)/shard_map/all_gather | solution.py:337
  397.6 53.1 %factor_2.1 = (f32[4,256,256]{2,1,0:T(8,128)}, bf16[768,1024]{1,0:T(8,128)(2,1)}) custom-call(s32[384]{0:T(512)} %reshape.20.map_ref, s32[768]{0:T(1024)} %reshape.21.mask_ref, f32[4,256,1024]{2,1,0:T(8,128)} %bitcast.28, bf16[3,256,3072]{2,1,0:T(8,128)(2,1)} %update_1.1.own_ref.refs_2_.refs_4_.refs_6_, ...), custom_call_target="tpu_custom_call" | custom-call | tf_op jit(solution)/shard_map/factor_2/pallas_call | solution.py:244
  450.8 68.7 %all-gather.15.cloned.1.call-done = bf16[3072,1024]{1,0:T(8,128)(2,1)} async-done(((bf16[768,1024]{1,0:T(8,128)(2,1)}), bf16[3072,1024]{1,0:T(8,128)(2,1)}) %all-gather.15.cloned.1.call-update) | async-done | bytes 6291472 | tf_op jit(solution)/shard_map/all_gather | solution.py:339
  519.5 6.4 %update_2.1 = bf16[3,256,768]{2,1,0:T(8,128)(2,1)} custom-call(s32[2]{0:T(128)} %pad_add_fusion.place_ref, s32[384]{0:T(512)} %reshape.20.map_ref, bf16[768,1024]{1,0:T(8,128)(2,1)} %get-tuple-element.10.refs_0_, bf16[4,768,1024]{2,1,0:T(8,128)(2,1)} %bitcast.26, bf16[3,256,3072]{2,1,0:T(8,128)(2,1)} %update_1.1.own_ref.refs_2_.refs_4_.refs_6_, ...), custom_call_target="tpu_custom_call" | custom-call | tf_op jit(solution)/shard_map/update_2/pallas_call | solution.py:311
  (20 shorter events, 0.2 us)
Async XLA Ops:
  7.2 69.2 %all-gather.9.cloned.1.call-start = ((), (), s32[]{:S(2)}) async-start(), calls=%async_computation | async-start | bytes 5242880 | tf_op jit(solution)/shard_map/all_gather | solution.py:337
  7.2 12.7 %collective-permute-start = (bf16[3,256,3072]{2,1,0:T(8,128)(2,1)}, bf16[3,256,3072]{2,1,0:T(8,128)(2,1)}, u32[]{:S(2)}, u32[]{:S(2)}) collective-permute-start(bf16[3,256,3072]{2,1,0:T(8,128)(2,1)} %bitcast.20), channel_id=1, source_target_pairs={{0,4},{4,0},{8,12},{12,8},{16,20},{20,16},{24,28},{28,24},{32,36},... | collective-permute-start | bytes 14155784 | tf_op jit(solution)/shard_map/ppermute | solution.py:25
  10.5 8.9 %collective-permute-start.1 = (bf16[4,256,512]{2,1,0:T(8,128)(2,1)}, bf16[4,256,512]{2,1,0:T(8,128)(2,1)S(1)}, u32[]{:S(2)}, u32[]{:S(2)}) collective-permute-start(bf16[4,256,512]{2,1,0:T(8,128)(2,1)} %bitcast.29), channel_id=1, source_target_pairs={{0,4},{4,0},{8,12},{12,8},{16,20},{20,16},{24,28},{28,24},{32,36},... | collective-permute-start | bytes 3145736 | tf_op jit(solution)/shard_map/ppermute | solution.py:25
  12.3 12.4 %copy-start.4 = (s32[32,1,12,4]{0,3,2,1:T(4,128)S(1)}, s32[32,1,12,4]{0,3,2,1:T(4,128)}, u32[]{:S(2)}) copy-start(s32[32,1,12,4]{0,3,2,1:T(4,128)} %param.12) | copy-start | bytes 18436
  19.4 1.0 copy-start.1
  24.6 174.0 %all-gather.11.cloned.1.call-start = ((), (), s32[]{:S(2)}) async-start(), calls=%async_computation.1 | async-start | bytes 7864320 | tf_op jit(solution)/shard_map/all_gather | solution.py:339
  129.9 267.7 %all-gather.13.cloned.1.call-start = ((), (), s32[]{:S(2)}) async-start(), calls=%async_computation.2 | async-start | bytes 5242880 | tf_op jit(solution)/shard_map/all_gather | solution.py:337
  198.6 17.1 %copy-start.3 = (bf16[1,1,1,4,256,256]{5,4,3,2,1,0:T(8,128)(2,1)S(1)}, bf16[1,1,1,4,256,256]{5,4,3,2,1,0:T(8,128)(2,1)}, u32[]{:S(2)}) copy-start(bf16[1,1,1,4,256,256]{5,4,3,2,1,0:T(8,128)(2,1)} %param.9) | copy-start | bytes 1572868
  214.5 4.3 copy-start.6
  214.5 125.3 %collective-permute-start.2 = (bf16[3,256,3072]{2,1,0:T(8,128)(2,1)}, bf16[3,256,3072]{2,1,0:T(8,128)(2,1)}, u32[]{:S(2)}, u32[]{:S(2)}) collective-permute-start(bf16[3,256,3072]{2,1,0:T(8,128)(2,1)} %update_1.1.own_ref.refs_2_.refs_4_.refs_6_), channel_id=1, source_target_pairs={{0,8},{4,12},{8,0},{12,4},{16,24},{20,28},{24,16},{28,20},{32,40},... | collective-permute-start | bytes 14155784 | tf_op jit(solution)/shard_map/ppermute | solution.py:25
  215.8 2.5 collective-permute-start.3
  218.5 121.3 %copy-start = (bf16[4,256,512]{2,1,0:T(8,128)(2,1)}, bf16[4,256,512]{2,1,0:T(8,128)(2,1)S(1)}, u32[]{:S(2)}) copy-start(bf16[4,256,512]{2,1,0:T(8,128)(2,1)S(1)} %maximum_select_fusion.init_own) | copy-start | bytes 3145732
  218.5 121.3 %collective-permute-start.4 = (bf16[4,256,512]{2,1,0:T(8,128)(2,1)S(1)}, bf16[4,256,512]{2,1,0:T(8,128)(2,1)S(1)}, u32[]{:S(2)}, u32[]{:S(2)}) collective-permute-start(bf16[4,256,512]{2,1,0:T(8,128)(2,1)S(1)} %maximum_select_fusion.init_own), channel_id=1, source_target_pairs={{0,8},{4,12},{8,0},{12,4},{16,24},{20,28},{24,16},{28,20},{32,40},... | collective-permute-start | bytes 3145736 | tf_op jit(solution)/shard_map/ppermute | solution.py:25
  219.7 125.4 %copy-start.5 = (s32[16,1,12,4]{0,3,2,1:T(4,128)S(1)}, s32[16,1,12,4]{0,3,2,1:T(4,128)}, u32[]{:S(2)}) copy-start(s32[16,1,12,4]{0,3,2,1:T(4,128)} %param.13) | copy-start | bytes 9220
  339.8 1.0 copy-start.2
  345.1 174.4 %all-gather.15.cloned.1.call-start = ((), (), s32[]{:S(2)}) async-start(), calls=%async_computation.3 | async-start | bytes 7864320 | tf_op jit(solution)/shard_map/all_gather | solution.py:339
Sparse Core Ops, SparseCore 0:
  24.8 51.5 all-gather.8
  130.0 68.5 all-gather.10
  345.2 52.3 all-gather.12
  450.9 68.5 all-gather.14

commit v2 on v1

v2 whole, which is shorter than its diff:
```python
import functools

import jax
import jax.numpy as jnp
from jax import lax
from jax.experimental import pallas as pl
from jax.experimental.pallas import tpu as pltpu
from jax.sharding import PartitionSpec as P

TILE = 256
ST = 4
UT = 12
RING = 4
S = 1024
U = 3072
C = 768
G = 128
F32 = jnp.float32
BF16 = jnp.bfloat16
VMEM_LIMIT = 60 * 1024 * 1024


def swapped(value, axis, apart):
    mask = 2**apart
    pairs = [(source, source ^ mask) for source in range(lax.axis_size(axis))]
    return lax.ppermute(value, axis, pairs)


def dot_nt(x, y):
    return lax.dot_general(x, y, (((1,), (1,)), ((), ())), preferred_element_type=F32)


def split(x):
    high = x.astype(BF16)
    return high, (x - high.astype(F32)).astype(BF16)


def left_parts(x):
    high, low = split(x)
    return jnp.concatenate([high, low, high], axis=1)


def right_parts(x):
    high, low = split(x)
    return jnp.concatenate([high, high, low], axis=1)


def source_of(map_ref, base, group, slot):
    first = map_ref[base + group * 3] == slot
    second = map_ref[base + group * 3 + 1] == slot
    third = map_ref[base + group * 3 + 2] == slot
    index = jnp.where(first, 0, jnp.where(second, 1, 2))
    live = jnp.logical_or(first, jnp.logical_or(second, third))
    return index, live


def invert_diagonal(block_ref, inverse_ref):
    sub = lax.broadcasted_iota(jnp.int32, (8, G), 0)
    lane = lax.broadcasted_iota(jnp.int32, (8, G), 1)
    slabs = G // 8
    rest = [block_ref[8 * r : 8 * r + 8, :] for r in range(slabs)]
    unit = [jnp.where(lane == sub + 8 * r, 1.0, 0.0).astype(F32) for r in range(slabs)]

    def lanes(v, c):
        return jnp.broadcast_to(v[:, c : c + 1], (8, G))

    def rows(v, i):
        return jnp.broadcast_to(v[i : i + 1, :], (8, G))

    for t in range(slabs):
        k = 8 * t
        cols = [lanes(rest[t], k + i) for i in range(8)]
        a = {(i, j): rows(cols[j], i) for j in range(8) for i in range(j, 8)}
        low = {}
        scale = []
        for i in range(8):
            scale.append(lax.rsqrt(a[i, i]))
            for j in range(i + 1, 8):
                low[j, i] = a[j, i] * scale[i]
            for j in range(i + 1, 8):
                for m in range(j, 8):
                    a[m, j] = a[m, j] - low[m, i] * low[j, i]

        def forward(pick):
            out = []
            for i in range(8):
                x = pick(i)
                for j in range(i):
                    x = x - low[i, j] * out[j]
                out.append(x * scale[i])
            return out

        upper = forward(lambda i: rows(rest[t], i))
        inv = forward(lambda i: rows(unit[t], i))
        packed = inv[0]
        for i in range(1, 8):
            packed = jnp.where(sub == i, inv[i], packed)
        inverse_ref[k : k + 8, :] = packed
        for r in range(t + 1, slabs):
            column = []
            for i in range(8):
                x = lanes(rest[r], k + i)
                for j in range(i):
                    x = x - column[j] * low[i, j]
                column.append(x * scale[i])
            for i in range(8):
                rest[r] = rest[r] - column[i] * upper[i]
                unit[r] = unit[r] - column[i] * inv[i]


def place():
    return lax.axis_index("leaf"), lax.axis_index("front")


def spread_kernel(map_ref, child_ref, out_ref, sems):
    leaf, group = place()
    copies = []
    for m in range(4):
        row, row_live = source_of(map_ref, leaf * UT, group, m)
        for c in range(ST):
            col, col_live = source_of(map_ref, leaf * UT, c, 0)
            start = pl.multiple_of((col * 4 + c) * TILE, TILE)
            there = slice(c * TILE, (c + 1) * TILE)
            copy = pltpu.make_async_copy(
                child_ref.at[row, :, pl.ds(start, TILE)], out_ref.at[m, :, there], sems.at[m, c]
            )
            copy.start()
            copies.append((copy, m, there, jnp.logical_and(row_live, col_live)))
    for copy, m, there, live in copies:
        copy.wait()

        @pl.when(jnp.logical_not(live))
        def _():
            out_ref[m, :, there] = jnp.zeros((TILE, TILE), BF16)


def spread(tile_map, child):
    return pl.pallas_call(
        spread_kernel,
        out_shape=jax.ShapeDtypeStruct((4, TILE, S), BF16),
        in_specs=[pl.BlockSpec(memory_space=pltpu.SMEM), pl.BlockSpec(memory_space=pl.ANY)],
        scratch_shapes=[pltpu.SemaphoreType.DMA((4, ST))],
        name="spread",
    )(tile_map, child)


def initial_kernel(level, mask_ref, own_ref, peer_ref, out_ref):
    leaf, group = place()
    front = leaf // (2 * level)
    half = (leaf // level) % 2
    for m in range(4):
        for c in range(ST):
            at = (m, slice(None), slice((c % 2) * TILE, (c % 2 + 1) * TILE))
            value = jnp.where(half == c // 2, own_ref[at].astype(F32), peer_ref[at].astype(F32))
            if m > 0:
                value = value * mask_ref[(front * UT + (m - 1) * 4 + group) * ST + c].astype(F32)
            out_ref[m, :, c * TILE : (c + 1) * TILE] = value.astype(BF16)


def initial(level, tile_mask, own, peer):
    vmem = pl.BlockSpec(memory_space=pltpu.VMEM)
    return pl.pallas_call(
        functools.partial(initial_kernel, level),
        out_shape=jax.ShapeDtypeStruct((4, TILE, S), BF16),
        in_specs=[pl.BlockSpec(memory_space=pltpu.SMEM), vmem, vmem],
        name=f"initial_{level}",
    )(tile_mask, own, peer)


def meet(devices):
    barrier = pltpu.get_barrier_semaphore()
    for device in devices:
        pl.semaphore_signal(
            barrier, inc=1, device_id=device, device_id_type=pl.DeviceIdType.MESH
        )
    pl.semaphore_wait(barrier, len(devices))


def remote(source, target, sems, slot, device):
    return pltpu.make_async_remote_copy(
        src_ref=source,
        dst_ref=target,
        send_sem=sems.at[0, slot],
        recv_sem=sems.at[1, slot],
        device_id=device,
        device_id_type=pl.DeviceIdType.MESH,
    )


def ring(buf, low, size, sems, slot, sibling):
    leaf, me = place()
    right, left, across = lax.rem(me + 1, RING), lax.rem(me + 3, RING), lax.rem(me + 2, RING)
    to_right, to_left = {"front": right}, {"front": left}
    part = size // 2
    first, second, whole = pl.ds(low, part), pl.ds(low + part, part), pl.ds(low, size)

    def send(source, rows, device, k):
        copy = remote(buf.at[source, rows], buf.at[source, rows], sems, slot + k, device)
        copy.start()
        return copy

    right_1 = send(me, first, to_right, 0)
    left_1 = send(me, second, to_left, 1)
    right_2 = send(me, second, to_right, 2)
    left_2 = send(me, first, to_left, 3)
    others = []
    if sibling is not None:
        others.append(send(me, whole, sibling, 6))
    right_1.wait_recv()
    right_3 = send(left, first, to_right, 4)
    left_1.wait_recv()
    left_3 = send(right, second, to_left, 5)
    right_2.wait_recv()
    if sibling is not None:
        others.append(send(left, whole, sibling, 7))
    left_2.wait_recv()
    if sibling is not None:
        others.append(send(right, whole, sibling, 8))
    right_3.wait_recv()
    left_3.wait_recv()
    if sibling is not None:
        others.append(send(across, whole, sibling, 9))
    for copy in others:
        copy.wait_recv()
    for copy in [right_1, left_1, right_2, left_2, right_3, left_3, *others]:
        copy.wait_send()


def neighbours():
    _, me = place()
    return [{"front": lax.rem(me + 1, RING)}, {"front": lax.rem(me + 3, RING)}]


def exchange_kernel(
    level, near_ref, init_ref, pivots_ref, far_ref, near_buf, init_buf, far_buf, sems, local_sems
):
    leaf, me = place()
    core = lax.rem(leaf, 2)
    sibling = {"leaf": leaf + 1 - 2 * core}
    bit = lax.rem(leaf // level, 2)
    partner = {"leaf": leaf + level * (1 - 2 * bit)}
    meet(neighbours() + [sibling] + ([partner] if level == 2 else []))
    half = TILE // 2
    low = pl.multiple_of(core * half, half)
    mine = pl.ds(low, half)
    theirs = mine if level == 2 else pl.ds(pl.multiple_of(half - low, half), half)
    pivot_copy = remote(near_ref.at[0, theirs], far_buf, sems, 10, partner)
    pivot_copy.start()
    if level == 1:
        coupling = remote(near_ref.at[pl.ds(1, 3)], far_ref, sems, 11, partner)
    else:
        coupling = remote(near_ref.at[pl.ds(1, 3), mine], far_ref.at[:, mine], sems, 11, partner)
    coupling.start()
    near_copy = pltpu.make_async_copy(near_ref.at[0, mine], near_buf, local_sems.at[0])
    init_copy = pltpu.make_async_copy(init_ref.at[0, mine], init_buf, local_sems.at[1])
    near_copy.start()
    init_copy.start()
    near_copy.wait()
    init_copy.wait()
    pivot_copy.wait_recv()
    pivots_ref[me, mine] = (
        near_buf[...].astype(F32) + far_buf[...].astype(F32) + init_buf[...].astype(F32)
    )
    ring(pivots_ref, low, half, sems, 0, sibling)
    coupling.wait_recv()
    if level == 2:
        onward = remote(far_ref.at[:, mine], far_ref.at[:, mine], sems, 12, sibling)
        onward.start()
        onward.wait()
    pivot_copy.wait_send()
    coupling.wait_send()


def exchange(level, near, init):
    hbm = pl.BlockSpec(memory_space=pl.ANY)
    half = TILE // 2
    return pl.pallas_call(
        functools.partial(exchange_kernel, level),
        out_shape=[
            jax.ShapeDtypeStruct((RING, TILE, S), F32),
            jax.ShapeDtypeStruct((3, TILE, S), BF16),
        ],
        in_specs=[hbm, hbm],
        out_specs=[pl.BlockSpec(memory_space=pltpu.VMEM), hbm],
        scratch_shapes=[
            pltpu.VMEM((half, S), BF16),
            pltpu.VMEM((half, S), BF16),
            pltpu.VMEM((half, S), BF16),
            pltpu.SemaphoreType.DMA((2, 13)),
            pltpu.SemaphoreType.DMA((2,)),
        ],
        compiler_params=pltpu.CompilerParams(
            collective_id=level, has_side_effects=True, vmem_limit_bytes=VMEM_LIMIT
        ),
        name=f"exchange_{level}",
    )(near, init)


def gather_one_kernel(panel_ref, out_ref, sems, local_sem):
    leaf, me = place()
    core = lax.rem(leaf, 2)
    sibling = {"leaf": leaf + 1 - 2 * core}
    meet(neighbours() + [sibling])
    half = C // 2
    mine = pl.ds(pl.multiple_of(core * half, half), half)
    copy = pltpu.make_async_copy(panel_ref.at[mine], out_ref.at[me, mine], local_sem)
    copy.start()
    copy.wait()
    ring(out_ref, pl.multiple_of(core * half, half), half, sems, 0, sibling)


def gather_two_kernel(panel_ref, out_ref, sems, local_sem):
    leaf, me = place()
    meet(neighbours())
    quarter = lax.rem(leaf, 4)
    column = lax.rem(me + quarter, RING)
    tile = lax.min((3 * quarter + column) // 4, 2)
    rows = pl.ds(pl.multiple_of(tile * TILE, TILE), TILE)
    copy = pltpu.make_async_copy(panel_ref.at[rows], out_ref.at[me], local_sem)
    copy.start()
    copy.wait()
    ring(out_ref, 0, TILE, sems, 0, None)


def gather(level, panel):
    hbm = pl.BlockSpec(memory_space=pl.ANY)
    kernel = gather_one_kernel if level == 1 else gather_two_kernel
    return pl.pallas_call(
        kernel,
        out_shape=jax.ShapeDtypeStruct((RING, C if level == 1 else TILE, S), BF16),
        in_specs=[hbm],
        out_specs=hbm,
        scratch_shapes=[
            pltpu.SemaphoreType.DMA((2, 10 if level == 1 else 6)),
            pltpu.SemaphoreType.DMA,
        ],
        compiler_params=pltpu.CompilerParams(
            collective_id=2 + level, has_side_effects=True, vmem_limit_bytes=VMEM_LIMIT
        ),
        name=f"gather_{level}",
    )(panel)


def factor_kernel(
    level, pivot_ref, near_ref, far_ref, init_ref,
    factor_ref, panel_ref, a_ref, l_ref, xl_ref, xr_ref, inv_ref, parts, sems
):
    leaf, group = place()
    width = S // (2 * level)
    pivots = []
    for t in range(RING):
        copy = pltpu.make_async_copy(
            pivot_ref.at[t], a_ref.at[pl.ds(t * TILE, TILE)], sems.at[3 + t]
        )
        copy.start()
        pivots.append(copy)
    sides = [near_ref.at[pl.ds(1, 3)], far_ref, init_ref.at[pl.ds(1, 3)]]
    copies = []
    for k, side in enumerate(sides):
        copy = pltpu.make_async_copy(side, parts.at[k], sems.at[k])
        copy.start()
        copies.append(copy)
    for copy in pivots + copies:
        copy.wait()
    for m in range(3):
        a_ref[S + m * TILE : S + (m + 1) * TILE, :] = (
            parts[0, m].astype(F32) + parts[1, m].astype(F32) + parts[2, m].astype(F32)
        )

    def step(g, _):
        cols = pl.ds(pl.multiple_of(g * G, G), G)
        invert_diagonal(a_ref.at[cols, cols], inv_ref)
        inverse = right_parts(inv_ref[...])

        def panel(low, high):
            x = dot_nt(left_parts(a_ref[low:high, cols]), inverse)
            l_ref[low:high, cols] = x
            xl_ref[low:high, :] = left_parts(x)
            if low < S:
                xr_ref[low:high, :] = right_parts(x)

        @pl.when(g < 4)
        def _():
            panel(0, S // 2)

        panel(S // 2, S)
        panel(S, S + C)
        for block in range(ST):

            @pl.when(g < 2 * block + 1)
            def _():
                there = slice(block * TILE, (block + 1) * TILE)
                a_ref[block * TILE :, there] -= dot_nt(xl_ref[block * TILE :, :], xr_ref[there, :])

        return 0

    lax.fori_loop(0, S // G, step, 0)
    part = pl.ds(pl.multiple_of((leaf % (2 * level)) * width, width), width)
    row = lax.broadcasted_iota(jnp.int32, (TILE, width), 0) + group * TILE
    col = lax.broadcasted_iota(jnp.int32, (TILE, width), 1) + (leaf % (2 * level)) * width
    own_rows = l_ref[pl.ds(pl.multiple_of(group * TILE, TILE), TILE), part]
    factor_ref[0] = jnp.where(row >= col, own_rows, 0.0)
    for m in range(1, 4):
        factor_ref[m] = l_ref[S + (m - 1) * TILE : S + m * TILE, part]
    panel_ref[...] = l_ref[S:, :].astype(BF16)


def factor_rows(level, pivots, near, far, init):
    width = S // (2 * level)
    hbm = pl.BlockSpec(memory_space=pl.ANY)
    return pl.pallas_call(
        functools.partial(factor_kernel, level),
        out_shape=[
            jax.ShapeDtypeStruct((4, TILE, width), F32),
            jax.ShapeDtypeStruct((C, S), BF16),
        ],
        in_specs=[hbm] * 4,
        scratch_shapes=[
            pltpu.VMEM((S + C, S), F32),
            pltpu.VMEM((S + C, S), F32),
            pltpu.VMEM((S + C, 3 * G), BF16),
            pltpu.VMEM((S, 3 * G), BF16),
            pltpu.VMEM((G, G), F32),
            pltpu.VMEM((3, 3, TILE, S), BF16),
            pltpu.SemaphoreType.DMA((7,)),
        ],
        compiler_params=pltpu.CompilerParams(vmem_limit_bytes=VMEM_LIMIT),
        cost_estimate=pl.CostEstimate(
            flops=50_000_000_000, bytes_accessed=20_000_000, transcendentals=0
        ),
        name=f"factor_{level}",
    )(pivots, near, far, init)


def update_one_rows(map_one, map_two, panel, panels, own, peer):
    here = jnp.stack(place()).astype(jnp.int32)

    def column(i, here_ref, two_ref):
        quarter = here_ref[0] % 4
        across = (quarter + 2) % 4
        t = jnp.where(i < 4, i, jnp.where(i < 7, 3 * quarter + i, 3 * across + i - 3))
        tile, live = source_of(two_ref, (here_ref[0] // 2) * UT, t % 4, t // 4)
        return t % 4, tile, live

    def panel_block(i, here_ref, one_ref, two_ref):
        other, tile, _ = column(i, here_ref, two_ref)
        return (other, tile, 0)

    def tile_block(s, side, i, here_ref, one_ref, two_ref):
        other, tile, _ = column(i, here_ref, two_ref)
        base = (here_ref[0] ^ side) * UT
        row, _ = source_of(one_ref, base, here_ref[1], 1 + s)
        col, _ = source_of(one_ref, base, other, 1 + tile)
        return (row, 0, col * 4 + other)

    def kernel(here_ref, one_ref, two_ref, x_ref, y_ref, *refs):
        tiles, pivot_out, near_out, far_out, total_ref = refs[:6], *refs[6:]
        i = pl.program_id(0)
        other, tile, col_live = column(i, here_ref, two_ref)
        product = dot_nt(x_ref[...], y_ref[0])
        for s in range(3):
            total = -product[s * TILE : (s + 1) * TILE, :]
            for side in (0, 1):
                base = (here_ref[0] ^ side) * UT
                _, live_row = source_of(one_ref, base, here_ref[1], 1 + s)
                _, live_col = source_of(one_ref, base, other, 1 + tile)
                live = jnp.logical_and(live_row, live_col)
                total = total + jnp.where(live, tiles[2 * s + side][0].astype(F32), 0.0)
            total_ref[s] = total.astype(BF16)

        def target(m):
            row, row_live = source_of(two_ref, (here_ref[0] // 2) * UT, here_ref[1], m)
            live = jnp.logical_and(row_live, col_live)
            return jnp.where(live, total_ref[row].astype(F32), 0.0).astype(BF16)

        @pl.when(i < 4)
        def _():
            for m in range(4):
                pivot_out[m] = target(m)

        @pl.when(jnp.logical_and(i >= 4, i < 7))
        def _():
            for m in range(1, 4):
                near_out[m - 1] = target(m)

        @pl.when(i >= 7)
        def _():
            for m in range(1, 4):
                far_out[m - 1] = target(m)

    return pl.pallas_call(
        kernel,
        out_shape=[
            jax.ShapeDtypeStruct((4, TILE, S), BF16),
            jax.ShapeDtypeStruct((3, TILE, C), BF16),
            jax.ShapeDtypeStruct((3, TILE, C), BF16),
        ],
        grid_spec=pltpu.PrefetchScalarGridSpec(
            num_scalar_prefetch=3,
            grid=(10,),
            in_specs=[
                pl.BlockSpec((C, S), lambda i, *_: (0, 0)),
                pl.BlockSpec((1, TILE, S), panel_block),
                *[
                    pl.BlockSpec((1, TILE, TILE), functools.partial(tile_block, s, side))
                    for s in range(3)
                    for side in (0, 1)
                ],
            ],
            out_specs=[
                pl.BlockSpec((4, TILE, TILE), lambda i, *_: (0, 0, jnp.minimum(i, 3))),
                pl.BlockSpec((3, TILE, TILE), lambda i, *_: (0, 0, jnp.clip(i - 4, 0, 2))),
                pl.BlockSpec((3, TILE, TILE), lambda i, *_: (0, 0, jnp.clip(i - 7, 0, 2))),
            ],
            scratch_shapes=[pltpu.VMEM((3, TILE, TILE), BF16)],
        ),
        compiler_params=pltpu.CompilerParams(vmem_limit_bytes=VMEM_LIMIT),
        name="update_1",
    )(here, map_one, map_two, panel, panels, *([own, peer] * 3))


def update_two_kernel(x_ref, y_ref, near_ref, far_ref, out_ref):
    leaf, _ = place()
    quarter = lax.rem(leaf, 4)
    for i in range(3):
        there = slice(i * TILE, (i + 1) * TILE)
        product = dot_nt(x_ref[...], y_ref[lax.rem(3 * quarter + i, RING)])
        for m in range(3):
            front = near_ref[m, :, there].astype(F32) + far_ref[m, :, there].astype(F32)
            out_ref[m, :, there] = (front - product[m * TILE : (m + 1) * TILE, :]).astype(BF16)


def update_two_rows(panel, panels, near, far):
    vmem = pl.BlockSpec(memory_space=pltpu.VMEM)
    return pl.pallas_call(
        update_two_kernel,
        out_shape=jax.ShapeDtypeStruct((3, TILE, C), BF16),
        in_specs=[vmem] * 4,
        compiler_params=pltpu.CompilerParams(vmem_limit_bytes=VMEM_LIMIT),
        name="update_2",
    )(panel, panels, near, far)


def join_halves(mine, other, position):
    lower_first = jnp.concatenate([mine, other], axis=-1)
    upper_first = jnp.concatenate([other, mine], axis=-1)
    return jnp.where(position == 0, lower_first, upper_first)


def body(child_update, sep_one, sep_two, map_one, map_two, mask_one, mask_two):
    leaf = lax.axis_index("leaf")
    own = child_update[0, 0, 0]
    entries = sep_one[0, 0, 0]
    quarter = sep_two[0, 0, 0]
    map_one, map_two = map_one.reshape(-1), map_two.reshape(-1)
    entries_peer, quarter_peer, peer = swapped((entries, quarter, own), "leaf", 0)
    near = spread(map_one, own)
    init = initial(1, mask_one.reshape(-1), entries, entries_peer)
    half = join_halves(quarter, quarter_peer, leaf % 2)
    pivots, far = exchange(1, near, init)
    half_far = swapped(half, "leaf", 1)
    factor_one, panel = factor_rows(1, pivots, near, far, init)
    panel, half, half_far = lax.optimization_barrier((panel, half, half_far))
    init_two = initial(2, mask_two.reshape(-1), half, half_far)
    panels = gather(1, panel)
    near, rest_near, rest_far = update_one_rows(map_one, map_two, panel, panels, own, peer)
    pivots, far = exchange(2, near, init_two)
    pivots, rest_far = lax.optimization_barrier((pivots, rest_far))
    rest_far = swapped(rest_far, "leaf", 1)
    factor_two, panel = factor_rows(2, pivots, near, far, init_two)
    panel, rest_far = lax.optimization_barrier((panel, rest_far))
    panels = gather(2, panel)
    update_two = update_two_rows(panel, panels, rest_near, rest_far)
    return (factor_one[None, None, None], factor_two[None, None, None], update_two[None, None, None])


def solution(mesh):
    split_spec = P("leaf", "front", None, None, None, None)
    return jax.shard_map(
        body,
        mesh=mesh,
        in_specs=(split_spec, split_spec, split_spec, P(), P(), P(), P()),
        out_specs=(split_spec, split_spec, split_spec),
        check_vma=False,
    )
```

time: 533 us -> 307 us (0.58)
  waiting for transfers between devices: 368 us -> 0.01 us
  Pallas kernels: 137 us -> 292 us
  between operations: 13.9 us -> 0.81 us
    all_gather x4 -> x0, waiting for transfers between devices: 239 us -> none  [the longest x2 137 us: level_step(): panels = lax.all_gather(panel, 'front', axis=0)]
    pallas_call x4 -> x9, Pallas kernels: 30.6 us -> 189 us  [the longest x2 94.5 us: gather(): pl.pallas_call(kernel, out_shape=jax.ShapeDtypeStruct((RING, C if level =...]
    ppermute x5, waiting for transfers between devices: 129 us -> 0.01 us  [swapped(): return lax.ppermute(value, axis, pairs)]
  transfers between devices with their start and end apart: 9 -> 5, of which waited for: 8 -> 0; matrix products, arithmetic and copies ran while one was open for 1% -> 2% of each run, Pallas kernels for 0% -> 65%
where the time goes in v2:
time: 307 us; the launch traced here: 306 us
  Pallas kernels  292 us (95%)
  local copies, waits for them, and re-layouts  7.47 us (2%)
  starting transfers between devices  4.84 us (2%)
    pallas_call x2, Pallas kernels, factor_rows(): pl.pallas_call(functools.partial(factor_kernel, level), out_shape=[jax.Sh...  103 us
    pallas_call x2, Pallas kernels, gather(): pl.pallas_call(kernel, out_shape=jax.ShapeDtypeStruct((RING, C if level =...  94.5 us
    pallas_call x2, Pallas kernels, exchange(): pl.pallas_call(functools.partial(exchange_kernel, level), out_shape=[jax....  62.4 us
    pallas_call x1, Pallas kernels, update_one_rows(): pl.pallas_call(kernel, out_shape=[jax.ShapeDtypeStruct((4, TILE, S), BF16...  15.7 us
    pallas_call x2, Pallas kernels, initial(): pl.pallas_call(functools.partial(initial_kernel, level), out_shape=jax.Sh...  7.1 us
  transfers between devices with their start and end apart: 5, of which 0 were waited for; matrix products, arithmetic and copies ran while one was open for 2% of the time, Pallas kernels for 65%

profile of v2, /device:TPU:1, one launch (start us, length us, event | category | flops | bytes accessed | tf_op | source)
XLA Modules:
  0.0 305.6 jit_solution(9197511174524840135)
XLA Ops:
  0.6 3.3 %collective-permute-start = (bf16[4,256,512]{2,1,0:T(8,128)(2,1)}, bf16[4,256,512]{2,1,0:T(8,128)(2,1)S(1)}, u32[]{:S(2)}, u32[]{:S(2)}) collective-permute-start(bf16[4,256,512]{2,1,0:T(8,128)(2,1)} %bitcast.22), channel_id=1, source_target_pairs={{0,4},{4,0},{8,12},{12,8},{16,20},{20,16},{24,28},{28,24},{32,36},... | collective-permute-start | bytes 3145736 | tf_op jit(solution)/shard_map/ppermute | solution.py:26
  4.0 0.1 collective-permute-start.1
  4.1 0.4 collective-permute-start.3
  4.5 0.8 copy.12
  5.3 0.8 reshape.20.two_ref
  6.1 0.8 copy.10
  6.9 0.8 reshape.18.map_ref.one_ref
  7.7 0.9 copy.13
  8.6 0.7 reshape.21.mask_ref
  9.3 0.9 copy.11
  10.2 0.7 reshape.19.mask_ref
  10.9 4.0 %spread.1.near_ref = bf16[4,256,1024]{2,1,0:T(8,128)(2,1)} custom-call(s32[768]{0:T(1024)} %reshape.18.map_ref.one_ref, bf16[3,256,3072]{2,1,0:T(8,128)(2,1)} %bitcast.17), custom_call_target="tpu_custom_call" | custom-call | tf_op jit(solution)/shard_map/spread/pallas_call | solution.py:138
  14.9 0.6 pad_add_fusion.here_ref
  15.6 0.2 maximum_select_fusion.own_ref
  15.8 0.0 copy-start
  15.9 0.3 collective-permute-start.2
  16.1 0.0 copy-start.3
  16.2 1.0 copy-done.3
  17.2 3.5 %initial_1.1.init_ref = bf16[4,256,1024]{2,1,0:T(8,128)(2,1)} custom-call(s32[1536]{0:T(1024)} %reshape.19.mask_ref, bf16[4,256,512]{2,1,0:T(8,128)(2,1)} %bitcast.23, bf16[4,256,512]{2,1,0:T(8,128)(2,1)} %copy-done.3), custom_call_target="tpu_custom_call" | custom-call | tf_op jit(solution)/shard_map/initial_1/pallas_call | solution.py:162
  20.7 27.5 %exchange_1.1 = (f32[4,256,1024]{2,1,0:T(8,128)}, bf16[3,256,1024]{2,1,0:T(8,128)(2,1)}) custom-call(bf16[4,256,1024]{2,1,0:T(8,128)(2,1)} %spread.1.near_ref, bf16[4,256,1024]{2,1,0:T(8,128)(2,1)} %initial_1.1.init_ref), custom_call_target="tpu_custom_call" | custom-call | tf_op jit(solution)/shard_map/exchange_1/pallas_call | solution.py:277
  48.2 51.5 %factor_1.1 = (f32[4,256,512]{2,1,0:T(8,128)}, bf16[768,1024]{1,0:T(8,128)(2,1)}) custom-call(f32[4,256,1024]{2,1,0:T(8,128)} %get-tuple-element.21.pivot_ref, bf16[4,256,1024]{2,1,0:T(8,128)(2,1)} %spread.1.near_ref, bf16[3,256,1024]{2,1,0:T(8,128)(2,1)} %get-tuple-element.22.far_ref, bf16[4,256,1024]{2,1,0:T(8,128)(2,1)} %initial_1.1.init_ref), custom_call_target="tpu_custom_call" | custom-call | flops 49999998976 | bytes 20000000 | tf_op jit(solution)/shard_map/factor_1/pallas_call | solution.py:411
  99.7 0.0 collective-permute-done.2.peer_ref
  99.8 0.0 copy-start.2
  99.8 57.3 %gather_1.1.y_ref = bf16[4,768,1024]{2,1,0:T(8,128)(2,1)} custom-call(bf16[768,1024]{1,0:T(8,128)(2,1)} %get-tuple-element.25.panel_ref.x_ref), custom_call_target="tpu_custom_call" | custom-call | tf_op jit(solution)/shard_map/gather_1/pallas_call | solution.py:328
  157.1 3.6 %initial_2.1.init_ref = bf16[4,256,1024]{2,1,0:T(8,128)(2,1)} custom-call(s32[768]{0:T(1024)} %reshape.21.mask_ref, bf16[4,256,512]{2,1,0:T(8,128)(2,1)} %copy-done, bf16[4,256,512]{2,1,0:T(8,128)(2,1)} %copy-done.2), custom_call_target="tpu_custom_call" | custom-call | tf_op jit(solution)/shard_map/initial_2/pallas_call | solution.py:162
  160.7 0.0 collective-permute-done.3.refs_1_.refs_3_.refs_5_
  160.7 15.7 %update_1.1 = (bf16[4,256,1024]{2,1,0:T(8,128)(2,1)}, bf16[3,256,768]{2,1,0:T(8,128)(2,1)}, bf16[3,256,768]{2,1,0:T(8,128)(2,1)}) custom-call(s32[2]{0:T(128)} %pad_add_fusion.here_ref, s32[768]{0:T(1024)} %reshape.18.map_ref.one_ref, s32[384]{0:T(512)} %reshape.20.two_ref, bf16[768,1024]{1,0:T(8,128)(2,1)} %get-tuple-element.25.panel_ref.x_ref, ...), custom_call_target="tpu_custom_call" | custom-call | tf_op jit(solution)/shard_map/update_1/pallas_call | solution.py:491
  176.4 34.9 %exchange_2.1 = (f32[4,256,1024]{2,1,0:T(8,128)}, bf16[3,256,1024]{2,1,0:T(8,128)(2,1)}) custom-call(bf16[4,256,1024]{2,1,0:T(8,128)(2,1)} %get-tuple-element.26.near_ref, bf16[4,256,1024]{2,1,0:T(8,128)(2,1)} %initial_2.1.init_ref), custom_call_target="tpu_custom_call" | custom-call | tf_op jit(solution)/shard_map/exchange_2/pallas_call | solution.py:277
  211.2 0.7 collective-permute-start.4
  212.0 51.2 %factor_2.1 = (f32[4,256,256]{2,1,0:T(8,128)}, bf16[768,1024]{1,0:T(8,128)(2,1)}) custom-call(f32[4,256,1024]{2,1,0:T(8,128)} %get-tuple-element.31.pivot_ref, bf16[4,256,1024]{2,1,0:T(8,128)(2,1)} %get-tuple-element.26.near_ref, bf16[3,256,1024]{2,1,0:T(8,128)(2,1)} %get-tuple-element.32.far_ref, bf16[4,256,1024]{2,1,0:T(8,128)(2,1)} %initial_2.1.init_ref), custom_call_target="tpu_custom_call" | custom-call | flops 49999998976 | bytes 20000000 | tf_op jit(solution)/shard_map/factor_2/pallas_call | solution.py:411
  263.2 37.2 %gather_2.1.y_ref = bf16[4,256,1024]{2,1,0:T(8,128)(2,1)} custom-call(bf16[768,1024]{1,0:T(8,128)(2,1)} %get-tuple-element.36.panel_ref.x_ref), custom_call_target="tpu_custom_call" | custom-call | tf_op jit(solution)/shard_map/gather_2/pallas_call | solution.py:328
  300.4 5.2 %update_2.1 = bf16[3,256,768]{2,1,0:T(8,128)(2,1)} custom-call(bf16[768,1024]{1,0:T(8,128)(2,1)} %get-tuple-element.36.panel_ref.x_ref, bf16[4,256,1024]{2,1,0:T(8,128)(2,1)} %gather_2.1.y_ref, bf16[3,256,768]{2,1,0:T(8,128)(2,1)} %get-tuple-element.37.near_ref, bf16[3,256,768]{2,1,0:T(8,128)(2,1)} %copy-done.1), custom_call_target="tpu_custom_call" | custom-call | tf_op jit(solution)/shard_map/update_2/pallas_call | solution.py:535
  (11 shorter events, 0.0 us)
Async XLA Ops:
  0.6 15.5 %collective-permute-start = (bf16[4,256,512]{2,1,0:T(8,128)(2,1)}, bf16[4,256,512]{2,1,0:T(8,128)(2,1)S(1)}, u32[]{:S(2)}, u32[]{:S(2)}) collective-permute-start(bf16[4,256,512]{2,1,0:T(8,128)(2,1)} %bitcast.22), channel_id=1, source_target_pairs={{0,4},{4,0},{8,12},{12,8},{16,20},{20,16},{24,28},{28,24},{32,36},... | collective-permute-start | bytes 3145736 | tf_op jit(solution)/shard_map/ppermute | solution.py:26
  4.0 11.6 %collective-permute-start.1 = (bf16[4,256,256]{2,1,0:T(8,128)(2,1)}, bf16[4,256,256]{2,1,0:T(8,128)(2,1)S(1)}, u32[]{:S(2)}, u32[]{:S(2)}) collective-permute-start(bf16[4,256,256]{2,1,0:T(8,128)(2,1)} %bitcast.24), channel_id=1, source_target_pairs={{0,4},{4,0},{8,12},{12,8},{16,20},{20,16},{24,28},{28,24},{32,36},... | collective-permute-start | bytes 1572872 | tf_op jit(solution)/shard_map/ppermute | solution.py:26
  4.1 156.6 %collective-permute-start.3 = (bf16[3,256,3072]{2,1,0:T(8,128)(2,1)}, bf16[3,256,3072]{2,1,0:T(8,128)(2,1)}, u32[]{:S(2)}, u32[]{:S(2)}) collective-permute-start(bf16[3,256,3072]{2,1,0:T(8,128)(2,1)} %bitcast.16), channel_id=1, source_target_pairs={{0,4},{4,0},{8,12},{12,8},{16,20},{20,16},{24,28},{28,24},{32,36},... | collective-permute-start | bytes 14155784 | tf_op jit(solution)/shard_map/ppermute | solution.py:26
  10.9 4.7 %copy-start.4 = (bf16[1,1,1,4,256,256]{5,4,3,2,1,0:T(8,128)(2,1)S(1)}, bf16[1,1,1,4,256,256]{5,4,3,2,1,0:T(8,128)(2,1)}, u32[]{:S(2)}) copy-start(bf16[1,1,1,4,256,256]{5,4,3,2,1,0:T(8,128)(2,1)} %param.9) | copy-start | bytes 1572868
  15.8 4.9 %copy-start = (bf16[4,256,512]{2,1,0:T(8,128)(2,1)}, bf16[4,256,512]{2,1,0:T(8,128)(2,1)S(1)}, u32[]{:S(2)}) copy-start(bf16[4,256,512]{2,1,0:T(8,128)(2,1)S(1)} %maximum_select_fusion.own_ref) | copy-start | bytes 3145732
  15.9 83.9 %collective-permute-start.2 = (bf16[4,256,512]{2,1,0:T(8,128)(2,1)S(1)}, bf16[4,256,512]{2,1,0:T(8,128)(2,1)S(1)}, u32[]{:S(2)}, u32[]{:S(2)}) collective-permute-start(bf16[4,256,512]{2,1,0:T(8,128)(2,1)S(1)} %maximum_select_fusion.own_ref), channel_id=1, source_target_pairs={{0,8},{4,12},{8,0},{12,4},{16,24},{20,28},{24,16},{28,20},{32,40},... | collective-permute-start | bytes 3145736 | tf_op jit(solution)/shard_map/ppermute | solution.py:26
  16.1 1.0 copy-start.3
  99.8 57.3 %copy-start.2 = (bf16[4,256,512]{2,1,0:T(8,128)(2,1)}, bf16[4,256,512]{2,1,0:T(8,128)(2,1)S(1)}, u32[]{:S(2)}) copy-start(bf16[4,256,512]{2,1,0:T(8,128)(2,1)S(1)} %collective-permute-done.2.peer_ref) | copy-start | bytes 3145732
  176.4 34.9 %copy-start.5 = (bf16[3,256,768]{2,1,0:T(8,128)(2,1)S(1)}, bf16[3,256,768]{2,1,0:T(8,128)(2,1)}, u32[]{:S(2)}) copy-start(bf16[3,256,768]{2,1,0:T(8,128)(2,1)} %get-tuple-element.35) | copy-start | bytes 3538948
  211.2 51.9 %collective-permute-start.4 = (bf16[3,256,768]{2,1,0:T(8,128)(2,1)S(1)}, bf16[3,256,768]{2,1,0:T(8,128)(2,1)S(1)}, u32[]{:S(2)}, u32[]{:S(2)}) collective-permute-start(bf16[3,256,768]{2,1,0:T(8,128)(2,1)S(1)} %copy-done.5), channel_id=1, source_target_pairs={{0,8},{4,12},{8,0},{12,4},{16,24},{20,28},{24,16},{28,20},{32,40},... | collective-permute-start | bytes 3538952 | tf_op jit(solution)/shard_map/ppermute | solution.py:26
  263.2 37.3 %copy-start.1 = (bf16[3,256,768]{2,1,0:T(8,128)(2,1)}, bf16[3,256,768]{2,1,0:T(8,128)(2,1)S(1)}, u32[]{:S(2)}) copy-start(bf16[3,256,768]{2,1,0:T(8,128)(2,1)S(1)} %collective-permute-done.4.far_ref) | copy-start | bytes 3538948

commit v3 on v2

--- a/solution.py
+++ b/solution.py
@@ -176,263 +176,355 @@
     pl.semaphore_wait(barrier, len(devices))
 
 
-def remote(source, target, sems, slot, device):
-    return pltpu.make_async_remote_copy(
-        src_ref=source,
-        dst_ref=target,
-        send_sem=sems.at[0, slot],
-        recv_sem=sems.at[1, slot],
-        device_id=device,
-        device_id_type=pl.DeviceIdType.MESH,
-    )
-
-
-def ring(buf, low, size, sems, slot, sibling):
-    leaf, me = place()
-    right, left, across = lax.rem(me + 1, RING), lax.rem(me + 3, RING), lax.rem(me + 2, RING)
-    to_right, to_left = {"front": right}, {"front": left}
-    part = size // 2
-    first, second, whole = pl.ds(low, part), pl.ds(low + part, part), pl.ds(low, size)
-
-    def send(source, rows, device, k):
-        copy = remote(buf.at[source, rows], buf.at[source, rows], sems, slot + k, device)
-        copy.start()
-        return copy
-
-    right_1 = send(me, first, to_right, 0)
-    left_1 = send(me, second, to_left, 1)
-    right_2 = send(me, second, to_right, 2)
-    left_2 = send(me, first, to_left, 3)
-    others = []
-    if sibling is not None:
-        others.append(send(me, whole, sibling, 6))
-    right_1.wait_recv()
-    right_3 = send(left, first, to_right, 4)
-    left_1.wait_recv()
-    left_3 = send(right, second, to_left, 5)
-    right_2.wait_recv()
-    if sibling is not None:
-        others.append(send(left, whole, sibling, 7))
-    left_2.wait_recv()
-    if sibling is not None:
-        others.append(send(right, whole, sibling, 8))
-    right_3.wait_recv()
-    left_3.wait_recv()
-    if sibling is not None:
-        others.append(send(across, whole, sibling, 9))
-    for copy in others:
-        copy.wait_recv()
-    for copy in [right_1, left_1, right_2, left_2, right_3, left_3, *others]:
-        copy.wait_send()
-
-
 def neighbours():
     _, me = place()
     return [{"front": lax.rem(me + 1, RING)}, {"front": lax.rem(me + 3, RING)}]
 
 
-def exchange_kernel(
-    level, near_ref, init_ref, pivots_ref, far_ref, near_buf, init_buf, far_buf, sems, local_sems
-):
+class Ring:
+    def __init__(self, view, size, sems, sibling, own):
+        _, me = place()
+        self.own = own
+        self.view, self.size, self.sems, self.sibling = view, size, sems, sibling
+        self.me = me
+        self.right, self.left = lax.rem(me + 1, RING), lax.rem(me + 3, RING)
+        self.across = lax.rem(me + 2, RING)
+
+    def copy(self, k, c):
+        part = self.size // 2
+        to_right, to_left = {"front": self.right}, {"front": self.left}
+        source, offset, rows, device = (
+            (self.me, 0, part, to_right),
+            (self.me, part, part, to_left),
+            (self.me, part, part, to_right),
+            (self.me, 0, part, to_left),
+            (self.left, 0, part, to_right),
+            (self.right, part, part, to_left),
+            (self.me, 0, self.size, self.sibling),
+            (self.left, 0, self.size, self.sibling),
+            (self.right, 0, self.size, self.sibling),
+            (self.across, 0, self.size, self.sibling),
+        )[k]
+        ref = self.view(source, offset, rows, c)
+        return pltpu.make_async_remote_copy(
+            src_ref=ref,
+            dst_ref=ref,
+            send_sem=self.sems.at[0, c, k],
+            recv_sem=self.sems.at[1, c, k],
+            device_id=device,
+            device_id_type=pl.DeviceIdType.MESH,
+        )
+
+    def begin(self, c):
+        for k in range(4):
+            self.copy(k, c).start()
+        if self.own:
+            self.copy(6, c).start()
+
+    def forward(self, c):
+        self.copy(0, c).wait_recv()
+        self.copy(4, c).start()
+        self.copy(1, c).wait_recv()
+        self.copy(5, c).start()
+        self.copy(2, c).wait_recv()
+        if self.sibling is not None:
+            self.copy(7, c).start()
+        self.copy(3, c).wait_recv()
+        if self.sibling is not None:
+            self.copy(8, c).start()
+
+    def finish(self, c):
+        self.copy(4, c).wait_recv()
+        self.copy(5, c).wait_recv()
+        if self.sibling is not None:
+            self.copy(9, c).start()
+
+    def settle(self, c):
+        for k in range(10 if self.sibling is not None else 6):
+            if k == 6 and not self.own:
+                continue
+            if k >= 6:
+                self.copy(k, c).wait_recv()
+            self.copy(k, c).wait_send()
+
+
+def front_kernel(level, near_ref, init_ref, factor_ref, *refs):
+    if level == 1:
+        panels_ref, *refs = refs
+    else:
+        panel_ref, panels_ref, *refs = refs
+    (a_ref, high_ref, low_ref, inv_ref, near_top, init_top, far_top, near_rest, init_rest, far_rest,
+     local_sems, top_sems, rest_sems, pivot_sems, panel_sems) = refs
     leaf, me = place()
     core = lax.rem(leaf, 2)
     sibling = {"leaf": leaf + 1 - 2 * core}
     bit = lax.rem(leaf // level, 2)
     partner = {"leaf": leaf + level * (1 - 2 * bit)}
-    meet(neighbours() + [sibling] + ([partner] if level == 2 else []))
     half = TILE // 2
     low = pl.multiple_of(core * half, half)
     mine = pl.ds(low, half)
     theirs = mine if level == 2 else pl.ds(pl.multiple_of(half - low, half), half)
-    pivot_copy = remote(near_ref.at[0, theirs], far_buf, sems, 10, partner)
-    pivot_copy.start()
+    quarter = lax.rem(leaf, 4)
+
+    def tile(c):
+        return pl.ds(pl.multiple_of(c * TILE, TILE), TILE)
+
+    loads = [
+        pltpu.make_async_copy(near_ref.at[0], near_top, local_sems.at[0]),
+        pltpu.make_async_copy(init_ref.at[0, mine], init_top, local_sems.at[1]),
+        pltpu.make_async_copy(near_ref.at[pl.ds(1, 3)], near_rest, local_sems.at[2]),
+        pltpu.make_async_copy(init_ref.at[pl.ds(1, 3)], init_rest, local_sems.at[3]),
+    ]
+    for load in loads:
+        load.start()
+    meet(neighbours() + [sibling] + ([partner] if level == 2 else []))
+
+    def top_copy(c):
+        return pltpu.make_async_remote_copy(
+            src_ref=near_top.at[theirs, tile(c)],
+            dst_ref=far_top.at[:, tile(c)],
+            send_sem=top_sems.at[0, c],
+            recv_sem=top_sems.at[1, c],
+            device_id=partner,
+            device_id_type=pl.DeviceIdType.MESH,
+        )
+
+    def rest_copy(c, k):
+        if level == 1:
+            source, target = near_rest.at[:, :, tile(c)], far_rest.at[:, :, tile(c)]
+        elif k == 0:
+            source, target = near_rest.at[:, mine, tile(c)], far_rest.at[:, mine, tile(c)]
+        else:
+            source = target = far_rest.at[:, mine, tile(c)]
+        return pltpu.make_async_remote_copy(
+            src_ref=source,
+            dst_ref=target,
+            send_sem=rest_sems.at[0, c, k],
+            recv_sem=rest_sems.at[1, c, k],
+            device_id=partner if k == 0 else sibling,
+            device_id_type=pl.DeviceIdType.MESH,
+        )
+
+    def rest_onward(c):
+        if level == 2:
+            rest_copy(c, 0).wait_recv()
+            rest_copy(c, 1).start()
+
+    pivots = Ring(
+        lambda source, offset, rows, c: a_ref.at[
+            pl.ds(pl.multiple_of(source * TILE + low + offset, half // 2), rows), tile(c)
+        ],
+        half,
+        pivot_sems,
+        sibling,
+        True,
+    )
+    share = C // 2 if level == 1 else TILE
+    base = core * share if level == 1 else 0
+    panels = Ring(
+        lambda source, offset, rows, c: panels_ref.at[
+            source, pl.ds(pl.multiple_of(base + offset, share // 2), rows), tile(c)
+        ],
+        share,
+        panel_sems,
+        sibling if level == 1 else None,
+        False,
+    )
+
+    loads[0].wait()
+    for c in range(ST):
+        top_copy(c).start()
+    loads[1].wait()
+    own_rows = pl.ds(pl.multiple_of(me * TILE + low, half), half)
+    for c in range(ST):
+        top_copy(c).wait_recv()
+        there = slice(c * TILE, (c + 1) * TILE)
+        a_ref[own_rows, there] = (
+            near_top[mine, there].astype(F32)
+            + far_top[:, there].astype(F32)
+            + init_top[:, there].astype(F32)
+        )
+        pivots.begin(c)
+    loads[2].wait()
+    loads[3].wait()
+    for c in range(ST):
+        rest_copy(c, 0).start()
+    pivots.forward(0)
+    rest_onward(0)
+    pivots.finish(0)
+
+    def arrive(c):
+        pivots.settle(c)
+        rest_copy(c, 0).wait_send()
+        if level == 2:
+            rest_copy(c, 1).wait()
+        else:
+            rest_copy(c, 0).wait_recv()
+        for m in range(3):
+            rows = slice(S + m * TILE, S + (m + 1) * TILE)
+            a_ref[rows, tile(c)] = (
+                near_rest[m, :, tile(c)].astype(F32)
+                + far_rest[m, :, tile(c)].astype(F32)
+                + init_rest[m, :, tile(c)].astype(F32)
+            )
+
+    def left(rows, cols):
+        return jnp.concatenate(
+            [high_ref[rows, cols], low_ref[rows, cols], high_ref[rows, cols]], axis=1
+        )
+
+    def right(rows, cols):
+        return jnp.concatenate(
+            [high_ref[rows, cols], high_ref[rows, cols], low_ref[rows, cols]], axis=1
+        )
+
+    def step(g, _):
+        c = g // 2
+        even = g % 2 == 0
+        odd = g % 2 == 1
+
+        @pl.when(even)
+        def _():
+            arrive(c)
+
+        for k in range(1, ST):
+
+            @pl.when(g == 2 * k)
+            def _():
+                rows, done = slice(k * TILE, None), slice(0, k * TILE)
+                there = slice(k * TILE, (k + 1) * TILE)
+                a_ref[rows, there] -= (
+                    dot_nt(high_ref[rows, done], high_ref[there, done])
+                    + dot_nt(low_ref[rows, done], high_ref[there, done])
+                    + dot_nt(high_ref[rows, done], low_ref[there, done])
+                )
+
+        cols = pl.ds(pl.multiple_of(g * G, G), G)
+        invert_diagonal(a_ref.at[cols, cols], inv_ref)
+
+        @pl.when(jnp.logical_and(even, g < 6))
+        def _():
+            pivots.forward(c + 1)
+            rest_onward(c + 1)
+
+        @pl.when(jnp.logical_and(odd, g < 6))
+        def _():
+            pivots.finish(c + 1)
+
+        @pl.when(jnp.logical_and(even, g > 1))
+        def _():
+            panels.forward(c - 1)
+
+        @pl.when(jnp.logical_and(odd, g > 1))
+        def _():
+            panels.finish(c - 1)
+
+        inverse = right_parts(inv_ref[...])
+
+        def panel(first, last):
+            x = dot_nt(left_parts(a_ref[first:last, cols]), inverse)
+            a_ref[first:last, cols] = x
+            high, rest = split(x)
+            high_ref[first:last, cols] = high
+            low_ref[first:last, cols] = rest
+
+        @pl.when(g < 4)
+        def _():
+            panel(0, S // 2)
+
+        panel(S // 2, S + C)
+
+        @pl.when(even)
+        def _():
+            after = pl.ds(pl.multiple_of(g * G + G, G), G)
+            y = right(after, cols)
+
+            def inside(first, last):
+                a_ref[first:last, after] -= dot_nt(left(slice(first, last), cols), y)
+
+            @pl.when(g < 4)
+            def _():
+                inside(0, S // 2)
+
+            inside(S // 2, S + C)
+
+        @pl.when(odd)
+        def _():
+            if level == 1:
+                panels_ref[me, :, tile(c)] = high_ref[S:, tile(c)]
+            else:
+                panel_ref[:, tile(c)] = high_ref[S:, tile(c)]
+                column = lax.rem(me + quarter, RING)
+                part = lax.min((3 * quarter + column) // 4, 2)
+                rows = pl.ds(pl.multiple_of(S + part * TILE, TILE), TILE)
+                panels_ref[me, :, tile(c)] = high_ref[rows, tile(c)]
+            panels.begin(c)
+
+        return 0
+
+    lax.fori_loop(0, S // G, step, 0)
+    panels.forward(ST - 1)
+    width = S // (2 * level)
+    start = lax.rem(leaf, 2 * level) * width
+    part = pl.ds(pl.multiple_of(start, width), width)
+    row = lax.broadcasted_iota(jnp.int32, (TILE, width), 0) + me * TILE
+    col = lax.broadcasted_iota(jnp.int32, (TILE, width), 1) + start
+    factor_ref[0] = jnp.where(row >= col, a_ref[tile(me), part], 0.0)
+    for m in range(1, 4):
+        factor_ref[m] = a_ref[S + (m - 1) * TILE : S + m * TILE, part]
+    panels.finish(ST - 1)
+    for c in range(ST):
+        panels.settle(c)
+        top_copy(c).wait_send()
+
+
+def front(level, near, init):
+    hbm = pl.BlockSpec(memory_space=pl.ANY)
+    vmem = pl.BlockSpec(memory_space=pltpu.VMEM)
+    width = S // (2 * level)
+    half = TILE // 2
+    factor = jax.ShapeDtypeStruct((4, TILE, width), F32)
     if level == 1:
-        coupling = remote(near_ref.at[pl.ds(1, 3)], far_ref, sems, 11, partner)
+        outs = [factor, jax.ShapeDtypeStruct((RING, C, S), BF16)]
     else:
-        coupling = remote(near_ref.at[pl.ds(1, 3), mine], far_ref.at[:, mine], sems, 11, partner)
-    coupling.start()
-    near_copy = pltpu.make_async_copy(near_ref.at[0, mine], near_buf, local_sems.at[0])
-    init_copy = pltpu.make_async_copy(init_ref.at[0, mine], init_buf, local_sems.at[1])
-    near_copy.start()
-    init_copy.start()
-    near_copy.wait()
-    init_copy.wait()
-    pivot_copy.wait_recv()
-    pivots_ref[me, mine] = (
-        near_buf[...].astype(F32) + far_buf[...].astype(F32) + init_buf[...].astype(F32)
-    )
-    ring(pivots_ref, low, half, sems, 0, sibling)
-    coupling.wait_recv()
-    if level == 2:
-        onward = remote(far_ref.at[:, mine], far_ref.at[:, mine], sems, 12, sibling)
-        onward.start()
-        onward.wait()
-    pivot_copy.wait_send()
-    coupling.wait_send()
-
-
-def exchange(level, near, init):
-    hbm = pl.BlockSpec(memory_space=pl.ANY)
-    half = TILE // 2
+        outs = [
+            factor,
+            jax.ShapeDtypeStruct((C, S), BF16),
+            jax.ShapeDtypeStruct((RING, TILE, S), BF16),
+        ]
     return pl.pallas_call(
-        functools.partial(exchange_kernel, level),
-        out_shape=[
-            jax.ShapeDtypeStruct((RING, TILE, S), F32),
-            jax.ShapeDtypeStruct((3, TILE, S), BF16),
-        ],
+        functools.partial(front_kernel, level),
+        out_shape=outs,
         in_specs=[hbm, hbm],
-        out_specs=[pl.BlockSpec(memory_space=pltpu.VMEM), hbm],
+        out_specs=[vmem] * len(outs),
         scratch_shapes=[
+            pltpu.VMEM((S + C, S), F32),
+            pltpu.VMEM((S + C, S), BF16),
+            pltpu.VMEM((S + C, S), BF16),
+            pltpu.VMEM((G, G), F32),
+            pltpu.VMEM((TILE, S), BF16),
             pltpu.VMEM((half, S), BF16),
             pltpu.VMEM((half, S), BF16),
-            pltpu.VMEM((half, S), BF16),
-            pltpu.SemaphoreType.DMA((2, 13)),
-            pltpu.SemaphoreType.DMA((2,)),
+            pltpu.VMEM((3, TILE, S), BF16),
+            pltpu.VMEM((3, TILE, S), BF16),
+            pltpu.VMEM((3, TILE, S), BF16),
+            pltpu.SemaphoreType.DMA((4,)),
+            pltpu.SemaphoreType.DMA((2, ST)),
+            pltpu.SemaphoreType.DMA((2, ST, 2)),
+            pltpu.SemaphoreType.DMA((2, ST, 10)),
+            pltpu.SemaphoreType.DMA((2, ST, 10)),
         ],
         compiler_params=pltpu.CompilerParams(
             collective_id=level, has_side_effects=True, vmem_limit_bytes=VMEM_LIMIT
         ),
-        name=f"exchange_{level}",
-    )(near, init)
-
-
-def gather_one_kernel(panel_ref, out_ref, sems, local_sem):
-    leaf, me = place()
-    core = lax.rem(leaf, 2)
-    sibling = {"leaf": leaf + 1 - 2 * core}
-    meet(neighbours() + [sibling])
-    half = C // 2
-    mine = pl.ds(pl.multiple_of(core * half, half), half)
-    copy = pltpu.make_async_copy(panel_ref.at[mine], out_ref.at[me, mine], local_sem)
-    copy.start()
-    copy.wait()
-    ring(out_ref, pl.multiple_of(core * half, half), half, sems, 0, sibling)
-
-
-def gather_two_kernel(panel_ref, out_ref, sems, local_sem):
-    leaf, me = place()
-    meet(neighbours())
-    quarter = lax.rem(leaf, 4)
-    column = lax.rem(me + quarter, RING)
-    tile = lax.min((3 * quarter + column) // 4, 2)
-    rows = pl.ds(pl.multiple_of(tile * TILE, TILE), TILE)
-    copy = pltpu.make_async_copy(panel_ref.at[rows], out_ref.at[me], local_sem)
-    copy.start()
-    copy.wait()
-    ring(out_ref, 0, TILE, sems, 0, None)
-
-
-def gather(level, panel):
-    hbm = pl.BlockSpec(memory_space=pl.ANY)
-    kernel = gather_one_kernel if level == 1 else gather_two_kernel
-    return pl.pallas_call(
-        kernel,
-        out_shape=jax.ShapeDtypeStruct((RING, C if level == 1 else TILE, S), BF16),
-        in_specs=[hbm],
-        out_specs=hbm,
-        scratch_shapes=[
-            pltpu.SemaphoreType.DMA((2, 10 if level == 1 else 6)),
-            pltpu.SemaphoreType.DMA,
-        ],
-        compiler_params=pltpu.CompilerParams(
-            collective_id=2 + level, has_side_effects=True, vmem_limit_bytes=VMEM_LIMIT
-        ),
-        name=f"gather_{level}",
-    )(panel)
-
-
-def factor_kernel(
-    level, pivot_ref, near_ref, far_ref, init_ref,
-    factor_ref, panel_ref, a_ref, l_ref, xl_ref, xr_ref, inv_ref, parts, sems
-):
-    leaf, group = place()
-    width = S // (2 * level)
-    pivots = []
-    for t in range(RING):
-        copy = pltpu.make_async_copy(
-            pivot_ref.at[t], a_ref.at[pl.ds(t * TILE, TILE)], sems.at[3 + t]
-        )
-        copy.start()
-        pivots.append(copy)
-    sides = [near_ref.at[pl.ds(1, 3)], far_ref, init_ref.at[pl.ds(1, 3)]]
-    copies = []
-    for k, side in enumerate(sides):
-        copy = pltpu.make_async_copy(side, parts.at[k], sems.at[k])
-        copy.start()
-        copies.append(copy)
-    for copy in pivots + copies:
-        copy.wait()
-    for m in range(3):
-        a_ref[S + m * TILE : S + (m + 1) * TILE, :] = (
-            parts[0, m].astype(F32) + parts[1, m].astype(F32) + parts[2, m].astype(F32)
-        )
-
-    def step(g, _):
-        cols = pl.ds(pl.multiple_of(g * G, G), G)
-        invert_diagonal(a_ref.at[cols, cols], inv_ref)
-        inverse = right_parts(inv_ref[...])
-
-        def panel(low, high):
-            x = dot_nt(left_parts(a_ref[low:high, cols]), inverse)
-            l_ref[low:high, cols] = x
-            xl_ref[low:high, :] = left_parts(x)
-            if low < S:
-                xr_ref[low:high, :] = right_parts(x)
-
-        @pl.when(g < 4)
-        def _():
-            panel(0, S // 2)
-
-        panel(S // 2, S)
-        panel(S, S + C)
-        for block in range(ST):
-
-            @pl.when(g < 2 * block + 1)
-            def _():
-                there = slice(block * TILE, (block + 1) * TILE)
-                a_ref[block * TILE :, there] -= dot_nt(xl_ref[block * TILE :, :], xr_ref[there, :])
-
-        return 0
-
-    lax.fori_loop(0, S // G, step, 0)
-    part = pl.ds(pl.multiple_of((leaf % (2 * level)) * width, width), width)
-    row = lax.broadcasted_iota(jnp.int32, (TILE, width), 0) + group * TILE
-    col = lax.broadcasted_iota(jnp.int32, (TILE, width), 1) + (leaf % (2 * level)) * width
-    own_rows = l_ref[pl.ds(pl.multiple_of(group * TILE, TILE), TILE), part]
-    factor_ref[0] = jnp.where(row >= col, own_rows, 0.0)
-    for m in range(1, 4):
-        factor_ref[m] = l_ref[S + (m - 1) * TILE : S + m * TILE, part]
-    panel_ref[...] = l_ref[S:, :].astype(BF16)
-
-
-def factor_rows(level, pivots, near, far, init):
-    width = S // (2 * level)
-    hbm = pl.BlockSpec(memory_space=pl.ANY)
-    return pl.pallas_call(
-        functools.partial(factor_kernel, level),
-        out_shape=[
-            jax.ShapeDtypeStruct((4, TILE, width), F32),
-            jax.ShapeDtypeStruct((C, S), BF16),
-        ],
-        in_specs=[hbm] * 4,
-        scratch_shapes=[
-            pltpu.VMEM((S + C, S), F32),
-            pltpu.VMEM((S + C, S), F32),
-            pltpu.VMEM((S + C, 3 * G), BF16),
-            pltpu.VMEM((S, 3 * G), BF16),
-            pltpu.VMEM((G, G), F32),
-            pltpu.VMEM((3, 3, TILE, S), BF16),
-            pltpu.SemaphoreType.DMA((7,)),
-        ],
-        compiler_params=pltpu.CompilerParams(vmem_limit_bytes=VMEM_LIMIT),
         cost_estimate=pl.CostEstimate(
             flops=50_000_000_000, bytes_accessed=20_000_000, transcendentals=0
         ),
-        name=f"factor_{level}",
-    )(pivots, near, far, init)
-
-
-def update_one_rows(map_one, map_two, panel, panels, own, peer):
+        name=f"front_{level}",
+    )(near, init)
+
+
+def update_one_rows(map_one, map_two, panels, own, peer):
     here = jnp.stack(place()).astype(jnp.int32)
 
     def column(i, here_ref, two_ref):
@@ -457,7 +549,7 @@
         tiles, pivot_out, near_out, far_out, total_ref = refs[:6], *refs[6:]
         i = pl.program_id(0)
         other, tile, col_live = column(i, here_ref, two_ref)
-        product = dot_nt(x_ref[...], y_ref[0])
+        product = dot_nt(x_ref[0], y_ref[0])
         for s in range(3):
             total = -product[s * TILE : (s + 1) * TILE, :]
             for side in (0, 1):
@@ -499,7 +591,7 @@
             num_scalar_prefetch=3,
             grid=(10,),
             in_specs=[
-                pl.BlockSpec((C, S), lambda i, *_: (0, 0)),
+                pl.BlockSpec((1, C, S), lambda i, here_ref, *_: (here_ref[1], 0, 0)),
                 pl.BlockSpec((1, TILE, S), panel_block),
                 *[
                     pl.BlockSpec((1, TILE, TILE), functools.partial(tile_block, s, side))
@@ -516,7 +608,7 @@
         ),
         compiler_params=pltpu.CompilerParams(vmem_limit_bytes=VMEM_LIMIT),
         name="update_1",
-    )(here, map_one, map_two, panel, panels, *([own, peer] * 3))
+    )(here, map_one, map_two, panels, panels, *([own, peer] * 3))
 
 
 def update_two_kernel(x_ref, y_ref, near_ref, far_ref, out_ref):
@@ -557,19 +649,14 @@
     near = spread(map_one, own)
     init = initial(1, mask_one.reshape(-1), entries, entries_peer)
     half = join_halves(quarter, quarter_peer, leaf % 2)
-    pivots, far = exchange(1, near, init)
     half_far = swapped(half, "leaf", 1)
-    factor_one, panel = factor_rows(1, pivots, near, far, init)
-    panel, half, half_far = lax.optimization_barrier((panel, half, half_far))
+    factor_one, panels = front(1, near, init)
+    panels, half, half_far = lax.optimization_barrier((panels, half, half_far))
     init_two = initial(2, mask_two.reshape(-1), half, half_far)
-    panels = gather(1, panel)
-    near, rest_near, rest_far = update_one_rows(map_one, map_two, panel, panels, own, peer)
-    pivots, far = exchange(2, near, init_two)
-    pivots, rest_far = lax.optimization_barrier((pivots, rest_far))
+    near, rest_near, rest_far = update_one_rows(map_one, map_two, panels, own, peer)
     rest_far = swapped(rest_far, "leaf", 1)
-    factor_two, panel = factor_rows(2, pivots, near, far, init_two)
+    factor_two, panel, panels = front(2, near, init_two)
     panel, rest_far = lax.optimization_barrier((panel, rest_far))
-    panels = gather(2, panel)
     update_two = update_two_rows(panel, panels, rest_near, rest_far)
     return (factor_one[None, None, None], factor_two[None, None, None], update_two[None, None, None])
 

time: 307 us -> 237 us (0.77)
  Pallas kernels: 292 us -> 218 us
  local copies, waits for them, and re-layouts: 7.47 us -> 12.4 us
    pallas_call x6 -> x2, Pallas kernels: 260 us -> 186 us  [front(): pl.pallas_call(functools.partial(front_kernel, level), out_shape=outs, in...]
    unnamed x16 -> x20, local copies, waits for them, and re-layouts: 4.45 us -> 9.34 us
  transfers between devices with their start and end apart: 5 -> 5, of which waited for: 0 -> 0; matrix products, arithmetic and copies ran while one was open for 2% -> 3% of each run, Pallas kernels for 65% -> 83%
where the time goes in v3:
time: 237 us; the launch traced here: 236 us
  Pallas kernels  218 us (92%)
  local copies, waits for them, and re-layouts  12.4 us (5%)
  starting transfers between devices  4.33 us (2%)
    pallas_call x2, Pallas kernels, front(): pl.pallas_call(functools.partial(front_kernel, level), out_shape=outs, in...  186 us
    pallas_call x1, Pallas kernels, update_one_rows(): pl.pallas_call(kernel, out_shape=[jax.ShapeDtypeStruct((4, TILE, S), BF16...  15.8 us
    unnamed x20, local copies, waits for them, and re-layouts  9.34 us
    pallas_call x2, Pallas kernels, initial(): pl.pallas_call(functools.partial(initial_kernel, level), out_shape=jax.Sh...  6.87 us
    pallas_call x1, Pallas kernels, update_two_rows(): pl.pallas_call(update_two_kernel, out_shape=jax.ShapeDtypeStruct((3, TILE...  5.31 us
  transfers between devices with their start and end apart: 5, of which 0 were waited for; matrix products, arithmetic and copies ran while one was open for 3% of the time, Pallas kernels for 83%

profile of v3, /device:TPU:1, one launch (start us, length us, event | category | flops | bytes accessed | tf_op | source)
XLA Modules:
  0.0 236.0 jit_solution(15307576533118344025)
XLA Ops:
  0.6 3.3 %collective-permute-start = (bf16[4,256,512]{2,1,0:T(8,128)(2,1)}, bf16[4,256,512]{2,1,0:T(8,128)(2,1)S(1)}, u32[]{:S(2)}, u32[]{:S(2)}) collective-permute-start(bf16[4,256,512]{2,1,0:T(8,128)(2,1)} %bitcast.24), channel_id=1, source_target_pairs={{0,4},{4,0},{8,12},{12,8},{16,20},{20,16},{24,28},{28,24},{32,36},... | collective-permute-start | bytes 3145736 | tf_op jit(solution)/shard_map/ppermute | solution.py:26
  4.0 0.1 collective-permute-start.1
  4.1 0.4 collective-permute-start.3
  4.5 0.8 copy.12
  5.3 0.8 reshape.20.two_ref
  6.1 0.8 copy.10
  6.9 0.8 reshape.18.map_ref.one_ref
  7.7 0.9 copy.13
  8.6 0.7 reshape.21.mask_ref
  9.3 0.9 copy.11
  10.2 0.7 reshape.19.mask_ref
  10.9 4.0 %spread.1.near_ref = bf16[4,256,1024]{2,1,0:T(8,128)(2,1)} custom-call(s32[768]{0:T(1024)} %reshape.18.map_ref.one_ref, bf16[3,256,3072]{2,1,0:T(8,128)(2,1)} %bitcast.17), custom_call_target="tpu_custom_call" | custom-call | tf_op jit(solution)/shard_map/spread/pallas_call | solution.py:138
  14.9 0.7 pad_add_fusion.here_ref
  15.6 0.2 maximum_select_fusion.own_ref
  15.8 0.0 copy-start
  15.9 0.3 collective-permute-start.2
  16.2 0.0 copy-start.5
  16.2 1.0 copy-done.5
  17.2 3.4 %initial_1.1.init_ref = bf16[4,256,1024]{2,1,0:T(8,128)(2,1)} custom-call(s32[1536]{0:T(1024)} %reshape.19.mask_ref, bf16[4,256,512]{2,1,0:T(8,128)(2,1)} %bitcast.25, bf16[4,256,512]{2,1,0:T(8,128)(2,1)} %copy-done.5), custom_call_target="tpu_custom_call" | custom-call | tf_op jit(solution)/shard_map/initial_1/pallas_call | solution.py:162
  20.6 83.9 %front_1.1 = (f32[4,256,512]{2,1,0:T(8,128)}, bf16[4,768,1024]{2,1,0:T(8,128)(2,1)}) custom-call(bf16[4,256,1024]{2,1,0:T(8,128)(2,1)} %spread.1.near_ref, bf16[4,256,1024]{2,1,0:T(8,128)(2,1)} %initial_1.1.init_ref), custom_call_target="tpu_custom_call" | custom-call | flops 49999998976 | bytes 20000000 | tf_op jit(solution)/shard_map/front_1/pallas_call | solution.py:495
  104.5 0.0 copy-start.3
  104.5 1.0 copy-done.3
  105.5 3.4 %initial_2.1.init_ref = bf16[4,256,1024]{2,1,0:T(8,128)(2,1)} custom-call(s32[768]{0:T(1024)} %reshape.21.mask_ref, bf16[4,256,512]{2,1,0:T(8,128)(2,1)} %copy-done, bf16[4,256,512]{2,1,0:T(8,128)(2,1)} %copy-done.3), custom_call_target="tpu_custom_call" | custom-call | tf_op jit(solution)/shard_map/initial_2/pallas_call | solution.py:162
  108.9 15.8 %update_1.1 = (bf16[4,256,1024]{2,1,0:T(8,128)(2,1)}, bf16[3,256,768]{2,1,0:T(8,128)(2,1)}, bf16[3,256,768]{2,1,0:T(8,128)(2,1)}) custom-call(s32[2]{0:T(128)} %pad_add_fusion.here_ref, s32[768]{0:T(1024)} %reshape.18.map_ref.one_ref, s32[384]{0:T(512)} %reshape.20.two_ref, bf16[4,768,1024]{2,1,0:T(8,128)(2,1)} %get-tuple-element.18.x_ref.y_ref, ...), custom_call_target="tpu_custom_call" | custom-call | tf_op jit(solution)/shard_map/update_1/pallas_call | solution.py:583
  124.7 0.2 collective-permute-start.4
  124.9 101.7 %front_2.1 = (f32[4,256,256]{2,1,0:T(8,128)}, bf16[768,1024]{1,0:T(8,128)(2,1)}, bf16[4,256,1024]{2,1,0:T(8,128)(2,1)}) custom-call(bf16[4,256,1024]{2,1,0:T(8,128)(2,1)} %get-tuple-element.19.near_ref, bf16[4,256,1024]{2,1,0:T(8,128)(2,1)} %initial_2.1.init_ref), custom_call_target="tpu_custom_call" | custom-call | flops 49999998976 | bytes 20000000 | tf_op jit(solution)/shard_map/front_2/pallas_call | solution.py:495
  226.7 0.0 copy-start.2
  226.7 1.0 copy-done.2
  227.7 5.3 %update_2.1 = bf16[3,256,768]{2,1,0:T(8,128)(2,1)} custom-call(bf16[768,1024]{1,0:T(8,128)(2,1)} %get-tuple-element.25.x_ref, bf16[4,256,1024]{2,1,0:T(8,128)(2,1)} %get-tuple-element.26.y_ref, bf16[3,256,768]{2,1,0:T(8,128)(2,1)} %get-tuple-element.27.near_ref, bf16[3,256,768]{2,1,0:T(8,128)(2,1)} %copy-done.2), custom_call_target="tpu_custom_call" | custom-call | tf_op jit(solution)/shard_map/update_2/pallas_call | solution.py:627
  233.0 1.3 copy.16
  234.3 0.6 copy-done.4
  235.0 1.0 copy.17
  (11 shorter events, 0.0 us)
Async XLA Ops:
  0.6 15.5 %collective-permute-start = (bf16[4,256,512]{2,1,0:T(8,128)(2,1)}, bf16[4,256,512]{2,1,0:T(8,128)(2,1)S(1)}, u32[]{:S(2)}, u32[]{:S(2)}) collective-permute-start(bf16[4,256,512]{2,1,0:T(8,128)(2,1)} %bitcast.24), channel_id=1, source_target_pairs={{0,4},{4,0},{8,12},{12,8},{16,20},{20,16},{24,28},{28,24},{32,36},... | collective-permute-start | bytes 3145736 | tf_op jit(solution)/shard_map/ppermute | solution.py:26
  4.0 11.6 %collective-permute-start.1 = (bf16[4,256,256]{2,1,0:T(8,128)(2,1)}, bf16[4,256,256]{2,1,0:T(8,128)(2,1)S(1)}, u32[]{:S(2)}, u32[]{:S(2)}) collective-permute-start(bf16[4,256,256]{2,1,0:T(8,128)(2,1)} %bitcast.26), channel_id=1, source_target_pairs={{0,4},{4,0},{8,12},{12,8},{16,20},{20,16},{24,28},{28,24},{32,36},... | collective-permute-start | bytes 1572872 | tf_op jit(solution)/shard_map/ppermute | solution.py:26
  4.1 104.9 %collective-permute-start.3 = (bf16[3,256,3072]{2,1,0:T(8,128)(2,1)}, bf16[3,256,3072]{2,1,0:T(8,128)(2,1)}, u32[]{:S(2)}, u32[]{:S(2)}) collective-permute-start(bf16[3,256,3072]{2,1,0:T(8,128)(2,1)} %bitcast.16), channel_id=1, source_target_pairs={{0,4},{4,0},{8,12},{12,8},{16,20},{20,16},{24,28},{28,24},{32,36},... | collective-permute-start | bytes 14155784 | tf_op jit(solution)/shard_map/ppermute | solution.py:26
  10.9 4.7 %copy-start.6 = (bf16[1,1,1,4,256,256]{5,4,3,2,1,0:T(8,128)(2,1)S(1)}, bf16[1,1,1,4,256,256]{5,4,3,2,1,0:T(8,128)(2,1)}, u32[]{:S(2)}) copy-start(bf16[1,1,1,4,256,256]{5,4,3,2,1,0:T(8,128)(2,1)} %param.9) | copy-start | bytes 1572868
  15.8 4.8 %copy-start = (bf16[4,256,512]{2,1,0:T(8,128)(2,1)}, bf16[4,256,512]{2,1,0:T(8,128)(2,1)S(1)}, u32[]{:S(2)}) copy-start(bf16[4,256,512]{2,1,0:T(8,128)(2,1)S(1)} %maximum_select_fusion.own_ref) | copy-start | bytes 3145732
  15.9 88.7 %collective-permute-start.2 = (bf16[4,256,512]{2,1,0:T(8,128)(2,1)S(1)}, bf16[4,256,512]{2,1,0:T(8,128)(2,1)S(1)}, u32[]{:S(2)}, u32[]{:S(2)}) collective-permute-start(bf16[4,256,512]{2,1,0:T(8,128)(2,1)S(1)} %maximum_select_fusion.own_ref), channel_id=1, source_target_pairs={{0,8},{4,12},{8,0},{12,4},{16,24},{20,28},{24,16},{28,20},{32,40},... | collective-permute-start | bytes 3145736 | tf_op jit(solution)/shard_map/ppermute | solution.py:26
  16.2 1.0 copy-start.5
  104.5 1.0 copy-start.3
  124.7 102.0 %collective-permute-start.4 = (bf16[3,256,768]{2,1,0:T(8,128)(2,1)}, bf16[3,256,768]{2,1,0:T(8,128)(2,1)S(1)}, u32[]{:S(2)}, u32[]{:S(2)}) collective-permute-start(bf16[3,256,768]{2,1,0:T(8,128)(2,1)} %get-tuple-element.24), channel_id=1, source_target_pairs={{0,8},{4,12},{8,0},{12,4},{16,24},{20,28},{24,16},{28,20},{32,40},... | collective-permute-start | bytes 3538952 | tf_op jit(solution)/shard_map/ppermute | solution.py:26
  226.7 1.0 copy-start.2
  227.7 5.3 %copy-start.1 = (f32[4,256,512]{2,1,0:T(8,128)S(1)}, f32[4,256,512]{2,1,0:T(8,128)}, u32[]{:S(2)}) copy-start(f32[4,256,512]{2,1,0:T(8,128)} %get-tuple-element.16) | copy-start | bytes 6291460
  233.0 2.0 copy-start.4

commit v4 on v3

--- a/solution.py
+++ b/solution.py
@@ -45,10 +45,10 @@
     return jnp.concatenate([high, high, low], axis=1)
 
 
-def source_of(map_ref, base, group, slot):
-    first = map_ref[base + group * 3] == slot
-    second = map_ref[base + group * 3 + 1] == slot
-    third = map_ref[base + group * 3 + 2] == slot
+def source_of(map_ref, child, group, slot):
+    first = map_ref[child, 0, group, 0] == slot
+    second = map_ref[child, 0, group, 1] == slot
+    third = map_ref[child, 0, group, 2] == slot
     index = jnp.where(first, 0, jnp.where(second, 1, 2))
     live = jnp.logical_or(first, jnp.logical_or(second, third))
     return index, live
@@ -116,9 +116,9 @@
     leaf, group = place()
     copies = []
     for m in range(4):
-        row, row_live = source_of(map_ref, leaf * UT, group, m)
+        row, row_live = source_of(map_ref, leaf, group, m)
         for c in range(ST):
-            col, col_live = source_of(map_ref, leaf * UT, c, 0)
+            col, col_live = source_of(map_ref, leaf, c, 0)
             start = pl.multiple_of((col * 4 + c) * TILE, TILE)
             there = slice(c * TILE, (c + 1) * TILE)
             copy = pltpu.make_async_copy(
@@ -144,29 +144,6 @@
     )(tile_map, child)
 
 
-def initial_kernel(level, mask_ref, own_ref, peer_ref, out_ref):
-    leaf, group = place()
-    front = leaf // (2 * level)
-    half = (leaf // level) % 2
-    for m in range(4):
-        for c in range(ST):
-            at = (m, slice(None), slice((c % 2) * TILE, (c % 2 + 1) * TILE))
-            value = jnp.where(half == c // 2, own_ref[at].astype(F32), peer_ref[at].astype(F32))
-            if m > 0:
-                value = value * mask_ref[(front * UT + (m - 1) * 4 + group) * ST + c].astype(F32)
-            out_ref[m, :, c * TILE : (c + 1) * TILE] = value.astype(BF16)
-
-
-def initial(level, tile_mask, own, peer):
-    vmem = pl.BlockSpec(memory_space=pltpu.VMEM)
-    return pl.pallas_call(
-        functools.partial(initial_kernel, level),
-        out_shape=jax.ShapeDtypeStruct((4, TILE, S), BF16),
-        in_specs=[pl.BlockSpec(memory_space=pltpu.SMEM), vmem, vmem],
-        name=f"initial_{level}",
-    )(tile_mask, own, peer)
-
-
 def meet(devices):
     barrier = pltpu.get_barrier_semaphore()
     for device in devices:
@@ -182,9 +159,9 @@
 
 
 class Ring:
-    def __init__(self, view, size, sems, sibling, own):
+    def __init__(self, view, size, sems, sibling, own, lower):
         _, me = place()
-        self.own = own
+        self.own, self.lower = own, lower
         self.view, self.size, self.sems, self.sibling = view, size, sems, sibling
         self.me = me
         self.right, self.left = lax.rem(me + 1, RING), lax.rem(me + 3, RING)
@@ -215,44 +192,67 @@
             device_id_type=pl.DeviceIdType.MESH,
         )
 
+    def sent(self, k):
+        return (
+            self.me, self.me, self.me, self.me, self.left, self.right,
+            self.me, self.left, self.right, self.across,
+        )[k]
+
+    def received(self, k):
+        return (
+            self.left, self.right, self.left, self.right, self.across, self.across,
+            self.me, self.left, self.right, self.across,
+        )[k]
+
+    def act(self, source, c, action):
+        if self.lower:
+            pl.when(source >= c)(action)
+        else:
+            action()
+
+    def start(self, k, c):
+        self.act(self.sent(k), c, lambda: self.copy(k, c).start())
+
+    def wait_recv(self, k, c):
+        self.act(self.received(k), c, lambda: self.copy(k, c).wait_recv())
+
+    def wait_send(self, k, c):
+        self.act(self.sent(k), c, lambda: self.copy(k, c).wait_send())
+
     def begin(self, c):
         for k in range(4):
-            self.copy(k, c).start()
+            self.start(k, c)
         if self.own:
-            self.copy(6, c).start()
+            self.start(6, c)
 
     def forward(self, c):
-        self.copy(0, c).wait_recv()
-        self.copy(4, c).start()
-        self.copy(1, c).wait_recv()
-        self.copy(5, c).start()
-        self.copy(2, c).wait_recv()
+        for k in range(4):
+            self.wait_recv(k, c)
+            if k < 2:
+                self.start(4 + k, c)
+            elif self.sibling is not None:
+                self.start(5 + k, c)
+
+    def finish(self, c):
+        self.wait_recv(4, c)
+        self.wait_recv(5, c)
         if self.sibling is not None:
-            self.copy(7, c).start()
-        self.copy(3, c).wait_recv()
-        if self.sibling is not None:
-            self.copy(8, c).start()
-
-    def finish(self, c):
-        self.copy(4, c).wait_recv()
-        self.copy(5, c).wait_recv()
-        if self.sibling is not None:
-            self.copy(9, c).start()
+            self.start(9, c)
 
     def settle(self, c):
         for k in range(10 if self.sibling is not None else 6):
             if k == 6 and not self.own:
                 continue
             if k >= 6:
-                self.copy(k, c).wait_recv()
-            self.copy(k, c).wait_send()
-
-
-def front_kernel(level, near_ref, init_ref, factor_ref, *refs):
+                self.wait_recv(k, c)
+            self.wait_send(k, c)
+
+
+def front_kernel(level, mask_ref, near_ref, own_ref, peer_ref, *refs):
     if level == 1:
-        panels_ref, *refs = refs
+        factor_ref, panels_ref, *refs = refs
     else:
-        panel_ref, panels_ref, *refs = refs
+        given_ref, factor_ref, panel_ref, panels_ref, taken_ref, given_buf, given_sems, *refs = refs
     (a_ref, high_ref, low_ref, inv_ref, near_top, init_top, far_top, near_rest, init_rest, far_rest,
      local_sems, top_sems, rest_sems, pivot_sems, panel_sems) = refs
     leaf, me = place()
@@ -271,10 +271,14 @@
 
     loads = [
         pltpu.make_async_copy(near_ref.at[0], near_top, local_sems.at[0]),
-        pltpu.make_async_copy(init_ref.at[0, mine], init_top, local_sems.at[1]),
-        pltpu.make_async_copy(near_ref.at[pl.ds(1, 3)], near_rest, local_sems.at[2]),
-        pltpu.make_async_copy(init_ref.at[pl.ds(1, 3)], init_rest, local_sems.at[3]),
+        pltpu.make_async_copy(own_ref.at[0, mine], init_top.at[bit], local_sems.at[1]),
+        pltpu.make_async_copy(peer_ref.at[0, mine], init_top.at[1 - bit], local_sems.at[2]),
+        pltpu.make_async_copy(near_ref.at[pl.ds(1, 3)], near_rest, local_sems.at[3]),
+        pltpu.make_async_copy(own_ref.at[pl.ds(1, 3)], init_rest.at[bit], local_sems.at[4]),
+        pltpu.make_async_copy(peer_ref.at[pl.ds(1, 3)], init_rest.at[1 - bit], local_sems.at[5]),
     ]
+    if level == 2:
+        loads.append(pltpu.make_async_copy(given_ref, given_buf, local_sems.at[6]))
     for load in loads:
         load.start()
     meet(neighbours() + [sibling] + ([partner] if level == 2 else []))
@@ -318,6 +322,7 @@
         pivot_sems,
         sibling,
         True,
+        True,
     )
     share = C // 2 if level == 1 else TILE
     base = core * share if level == 1 else 0
@@ -329,12 +334,24 @@
         panel_sems,
         sibling if level == 1 else None,
         False,
+        False,
     )
+
+    def give():
+        return pltpu.make_async_remote_copy(
+            src_ref=given_buf,
+            dst_ref=taken_ref,
+            send_sem=given_sems.at[0],
+            recv_sem=given_sems.at[1],
+            device_id=partner,
+            device_id_type=pl.DeviceIdType.MESH,
+        )
 
     loads[0].wait()
     for c in range(ST):
         top_copy(c).start()
     loads[1].wait()
+    loads[2].wait()
     own_rows = pl.ds(pl.multiple_of(me * TILE + low, half), half)
     for c in range(ST):
         top_copy(c).wait_recv()
@@ -342,14 +359,16 @@
         a_ref[own_rows, there] = (
             near_top[mine, there].astype(F32)
             + far_top[:, there].astype(F32)
-            + init_top[:, there].astype(F32)
+            + init_top[c // 2, :, (c % 2) * TILE : (c % 2 + 1) * TILE].astype(F32)
         )
-        pivots.begin(c)
-    loads[2].wait()
-    loads[3].wait()
+        if c == 0:
+            pivots.begin(0)
+    for load in loads[3:]:
+        load.wait()
     for c in range(ST):
         rest_copy(c, 0).start()
     pivots.forward(0)
+    pivots.begin(1)
     rest_onward(0)
     pivots.finish(0)
 
@@ -362,10 +381,11 @@
             rest_copy(c, 0).wait_recv()
         for m in range(3):
             rows = slice(S + m * TILE, S + (m + 1) * TILE)
+            keep = mask_ref[leaf // (2 * level), 0, 4 * m + me, c].astype(F32)
             a_ref[rows, tile(c)] = (
                 near_rest[m, :, tile(c)].astype(F32)
                 + far_rest[m, :, tile(c)].astype(F32)
-                + init_rest[m, :, tile(c)].astype(F32)
+                + init_rest[c // 2, m, :, tile(c % 2)].astype(F32) * keep
             )
 
     def left(rows, cols):
@@ -407,17 +427,19 @@
             pivots.forward(c + 1)
             rest_onward(c + 1)
 
+        @pl.when(jnp.logical_and(even, g < 4))
+        def _():
+            pivots.begin(c + 2)
+
+        if level == 2:
+
+            @pl.when(g == 4)
+            def _():
+                give().start()
+
         @pl.when(jnp.logical_and(odd, g < 6))
         def _():
             pivots.finish(c + 1)
-
-        @pl.when(jnp.logical_and(even, g > 1))
-        def _():
-            panels.forward(c - 1)
-
-        @pl.when(jnp.logical_and(odd, g > 1))
-        def _():
-            panels.finish(c - 1)
 
         inverse = right_parts(inv_ref[...])
 
@@ -447,6 +469,14 @@
                 inside(0, S // 2)
 
             inside(S // 2, S + C)
+
+        @pl.when(jnp.logical_and(even, g > 1))
+        def _():
+            panels.forward(c - 1)
+
+        @pl.when(jnp.logical_and(odd, g > 1))
+        def _():
+            panels.finish(c - 1)
 
         @pl.when(odd)
         def _():
@@ -476,9 +506,11 @@
     for c in range(ST):
         panels.settle(c)
         top_copy(c).wait_send()
-
-
-def front(level, near, init):
+    if level == 2:
+        give().wait()
+
+
+def front(level, tile_mask, near, own, peer, given=None):
     hbm = pl.BlockSpec(memory_space=pl.ANY)
     vmem = pl.BlockSpec(memory_space=pltpu.VMEM)
     width = S // (2 * level)
@@ -491,24 +523,27 @@
             factor,
             jax.ShapeDtypeStruct((C, S), BF16),
             jax.ShapeDtypeStruct((RING, TILE, S), BF16),
+            jax.ShapeDtypeStruct((3, TILE, C), BF16),
         ]
+    given = [] if level == 1 else [given]
     return pl.pallas_call(
         functools.partial(front_kernel, level),
         out_shape=outs,
-        in_specs=[hbm, hbm],
+        in_specs=[pl.BlockSpec(memory_space=pltpu.SMEM)] + [hbm] * (3 + len(given)),
         out_specs=[vmem] * len(outs),
         scratch_shapes=[
+            *([pltpu.VMEM((3, TILE, C), BF16), pltpu.SemaphoreType.DMA((2,))] if given else []),
             pltpu.VMEM((S + C, S), F32),
             pltpu.VMEM((S + C, S), BF16),
             pltpu.VMEM((S + C, S), BF16),
             pltpu.VMEM((G, G), F32),
             pltpu.VMEM((TILE, S), BF16),
-            pltpu.VMEM((half, S), BF16),
+            pltpu.VMEM((2, half, S // 2), BF16),
             pltpu.VMEM((half, S), BF16),
             pltpu.VMEM((3, TILE, S), BF16),
+            pltpu.VMEM((2, 3, TILE, S // 2), BF16),
             pltpu.VMEM((3, TILE, S), BF16),
-            pltpu.VMEM((3, TILE, S), BF16),
-            pltpu.SemaphoreType.DMA((4,)),
+            pltpu.SemaphoreType.DMA((7,)),
             pltpu.SemaphoreType.DMA((2, ST)),
             pltpu.SemaphoreType.DMA((2, ST, 2)),
             pltpu.SemaphoreType.DMA((2, ST, 10)),
@@ -521,94 +556,109 @@
             flops=50_000_000_000, bytes_accessed=20_000_000, transcendentals=0
         ),
         name=f"front_{level}",
-    )(near, init)
-
-
-def update_one_rows(map_one, map_two, panels, own, peer):
-    here = jnp.stack(place()).astype(jnp.int32)
-
-    def column(i, here_ref, two_ref):
-        quarter = here_ref[0] % 4
-        across = (quarter + 2) % 4
+    )(tile_mask, near, own, peer, *given)
+
+
+def update_one_kernel(one_ref, two_ref, panels_ref, own_ref, peer_ref, pivot_out, near_out, far_out,
+                      x_buf, y_buf, tiles, total_ref, sems, x_sem):
+    leaf, group = place()
+    quarter = leaf % 4
+    across = (quarter + 2) % 4
+    sides = (own_ref, peer_ref)
+
+    def column(i):
         t = jnp.where(i < 4, i, jnp.where(i < 7, 3 * quarter + i, 3 * across + i - 3))
-        tile, live = source_of(two_ref, (here_ref[0] // 2) * UT, t % 4, t // 4)
+        tile, live = source_of(two_ref, leaf // 2, t % 4, t // 4)
         return t % 4, tile, live
 
-    def panel_block(i, here_ref, one_ref, two_ref):
-        other, tile, _ = column(i, here_ref, two_ref)
-        return (other, tile, 0)
-
-    def tile_block(s, side, i, here_ref, one_ref, two_ref):
-        other, tile, _ = column(i, here_ref, two_ref)
-        base = (here_ref[0] ^ side) * UT
-        row, _ = source_of(one_ref, base, here_ref[1], 1 + s)
-        col, _ = source_of(one_ref, base, other, 1 + tile)
-        return (row, 0, col * 4 + other)
-
-    def kernel(here_ref, one_ref, two_ref, x_ref, y_ref, *refs):
-        tiles, pivot_out, near_out, far_out, total_ref = refs[:6], *refs[6:]
-        i = pl.program_id(0)
-        other, tile, col_live = column(i, here_ref, two_ref)
-        product = dot_nt(x_ref[0], y_ref[0])
+    def there(i):
+        return pl.ds(pl.multiple_of(i * TILE, TILE), TILE)
+
+    def copy(source, target, i, k):
+        return pltpu.make_async_copy(source, target, sems.at[i, k])
+
+    rows = [[source_of(one_ref, leaf ^ side, group, 1 + s) for s in range(3)] for side in (0, 1)]
+    targets = [source_of(two_ref, leaf // 2, group, m) for m in range(4)]
+    x_copy = pltpu.make_async_copy(panels_ref.at[group], x_buf, x_sem)
+    x_copy.start()
+
+    def start(i, _):
+        other, tile, _ = column(i)
+        copy(panels_ref.at[other, there(tile)], y_buf.at[i], i, 0).start()
+        for side in (0, 1):
+            col, _ = source_of(one_ref, leaf ^ side, other, 1 + tile)
+            for s in range(3):
+                copy(
+                    sides[side].at[rows[side][s][0], :, there(col * 4 + other)],
+                    tiles.at[side, s, :, there(i)],
+                    i,
+                    1 + 3 * side + s,
+                ).start()
+        return 0
+
+    lax.fori_loop(0, 10, start, 0)
+    x_copy.wait()
+
+    def step(i, _):
+        other, tile, col_live = column(i)
+        copy(panels_ref.at[0, there(0)], y_buf.at[i], i, 0).wait()
+        product = dot_nt(x_buf[...], y_buf[i])
         for s in range(3):
             total = -product[s * TILE : (s + 1) * TILE, :]
             for side in (0, 1):
-                base = (here_ref[0] ^ side) * UT
-                _, live_row = source_of(one_ref, base, here_ref[1], 1 + s)
-                _, live_col = source_of(one_ref, base, other, 1 + tile)
-                live = jnp.logical_and(live_row, live_col)
-                total = total + jnp.where(live, tiles[2 * s + side][0].astype(F32), 0.0)
+                slot = tiles.at[side, s, :, there(i)]
+                copy(own_ref.at[0, :, there(0)], slot, i, 1 + 3 * side + s).wait()
+                _, live = source_of(one_ref, leaf ^ side, other, 1 + tile)
+                live = jnp.logical_and(rows[side][s][1], live)
+                total = total + jnp.where(live, slot[...].astype(F32), 0.0)
             total_ref[s] = total.astype(BF16)
 
         def target(m):
-            row, row_live = source_of(two_ref, (here_ref[0] // 2) * UT, here_ref[1], m)
-            live = jnp.logical_and(row_live, col_live)
-            return jnp.where(live, total_ref[row].astype(F32), 0.0).astype(BF16)
+            live = jnp.logical_and(targets[m][1], col_live)
+            return jnp.where(live, total_ref[targets[m][0]].astype(F32), 0.0).astype(BF16)
 
         @pl.when(i < 4)
         def _():
             for m in range(4):
-                pivot_out[m] = target(m)
+                pivot_out[m, :, there(i)] = target(m)
 
         @pl.when(jnp.logical_and(i >= 4, i < 7))
         def _():
             for m in range(1, 4):
-                near_out[m - 1] = target(m)
+                near_out[m - 1, :, there(i - 4)] = target(m)
 
         @pl.when(i >= 7)
         def _():
             for m in range(1, 4):
-                far_out[m - 1] = target(m)
-
+                far_out[m - 1, :, there(i - 7)] = target(m)
+
+        return 0
+
+    lax.fori_loop(0, 10, step, 0)
+
+
+def update_one_rows(map_one, map_two, panels, own, peer):
+    smem = pl.BlockSpec(memory_space=pltpu.SMEM)
+    hbm = pl.BlockSpec(memory_space=pl.ANY)
     return pl.pallas_call(
-        kernel,
+        update_one_kernel,
         out_shape=[
             jax.ShapeDtypeStruct((4, TILE, S), BF16),
             jax.ShapeDtypeStruct((3, TILE, C), BF16),
             jax.ShapeDtypeStruct((3, TILE, C), BF16),
         ],
-        grid_spec=pltpu.PrefetchScalarGridSpec(
-            num_scalar_prefetch=3,
-            grid=(10,),
-            in_specs=[
-                pl.BlockSpec((1, C, S), lambda i, here_ref, *_: (here_ref[1], 0, 0)),
-                pl.BlockSpec((1, TILE, S), panel_block),
-                *[
-                    pl.BlockSpec((1, TILE, TILE), functools.partial(tile_block, s, side))
-                    for s in range(3)
-                    for side in (0, 1)
-                ],
-            ],
-            out_specs=[
-                pl.BlockSpec((4, TILE, TILE), lambda i, *_: (0, 0, jnp.minimum(i, 3))),
-                pl.BlockSpec((3, TILE, TILE), lambda i, *_: (0, 0, jnp.clip(i - 4, 0, 2))),
-                pl.BlockSpec((3, TILE, TILE), lambda i, *_: (0, 0, jnp.clip(i - 7, 0, 2))),
-            ],
-            scratch_shapes=[pltpu.VMEM((3, TILE, TILE), BF16)],
-        ),
+        in_specs=[smem, smem, hbm, hbm, hbm],
+        scratch_shapes=[
+            pltpu.VMEM((C, S), BF16),
+            pltpu.VMEM((10, TILE, S), BF16),
+            pltpu.VMEM((2, 3, TILE, 10 * TILE), BF16),
+            pltpu.VMEM((3, TILE, TILE), BF16),
+            pltpu.SemaphoreType.DMA((10, 7)),
+            pltpu.SemaphoreType.DMA,
+        ],
         compiler_params=pltpu.CompilerParams(vmem_limit_bytes=VMEM_LIMIT),
         name="update_1",
-    )(here, map_one, map_two, panels, panels, *([own, peer] * 3))
+    )(map_one, map_two, panels, own, peer)
 
 
 def update_two_kernel(x_ref, y_ref, near_ref, far_ref, out_ref):
@@ -644,20 +694,15 @@
     own = child_update[0, 0, 0]
     entries = sep_one[0, 0, 0]
     quarter = sep_two[0, 0, 0]
-    map_one, map_two = map_one.reshape(-1), map_two.reshape(-1)
     entries_peer, quarter_peer, peer = swapped((entries, quarter, own), "leaf", 0)
     near = spread(map_one, own)
-    init = initial(1, mask_one.reshape(-1), entries, entries_peer)
     half = join_halves(quarter, quarter_peer, leaf % 2)
     half_far = swapped(half, "leaf", 1)
-    factor_one, panels = front(1, near, init)
+    factor_one, panels = front(1, mask_one, near, entries, entries_peer)
     panels, half, half_far = lax.optimization_barrier((panels, half, half_far))
-    init_two = initial(2, mask_two.reshape(-1), half, half_far)
-    near, rest_near, rest_far = update_one_rows(map_one, map_two, panels, own, peer)
-    rest_far = swapped(rest_far, "leaf", 1)
-    factor_two, panel, panels = front(2, near, init_two)
-    panel, rest_far = lax.optimization_barrier((panel, rest_far))
-    update_two = update_two_rows(panel, panels, rest_near, rest_far)
+    near, rest, given = update_one_rows(map_one, map_two, panels, own, peer)
+    factor_two, panel, panels, taken = front(2, mask_two, near, half, half_far, given)
+    update_two = update_two_rows(panel, panels, rest, taken)
     return (factor_one[None, None, None], factor_two[None, None, None], update_two[None, None, None])
 
 

time: 237 us -> 203 us (0.86)
  Pallas kernels: 218 us -> 189 us
  local copies, waits for them, and re-layouts: 12.4 us -> 7.83 us
    pallas_call x2, Pallas kernels: 186 us -> 160 us  [front(): pl.pallas_call(functools.partial(front_kernel, level), out_shape=outs, in...]
    pallas_call x3 -> x1, Pallas kernels: 22.6 us -> 17.7 us  [update_one_rows(): pl.pallas_call(update_one_kernel, out_shape=[jax.ShapeDtypeStruct((4, TIL...]
    reshape x4 -> x0, local copies, waits for them, and re-layouts: 3.03 us -> none  [the longest x2 1.61 us: body(): map_one, map_two = (map_one.reshape(-1), map_two.reshape(-1))]
    unnamed x20 -> x24, local copies, waits for them, and re-layouts: 9.34 us -> 7.83 us
  transfers between devices with their start and end apart: 5 -> 4, of which waited for: 0 -> 0; matrix products, arithmetic and copies ran while one was open for 3% -> 2% of each run, Pallas kernels for 83% -> 43%
where the time goes in v4:
time: 203 us; the launch traced here: 202 us
  Pallas kernels  189 us (93%)
  local copies, waits for them, and re-layouts  7.83 us (4%)
  starting transfers between devices  4.11 us (2%)
    pallas_call x2, Pallas kernels, front(): pl.pallas_call(functools.partial(front_kernel, level), out_shape=outs, in...  160 us
    pallas_call x1, Pallas kernels, update_one_rows(): pl.pallas_call(update_one_kernel, out_shape=[jax.ShapeDtypeStruct((4, TIL...  17.7 us
    unnamed x24, local copies, waits for them, and re-layouts  7.83 us
    pallas_call x1, Pallas kernels, spread(): pl.pallas_call(spread_kernel, out_shape=jax.ShapeDtypeStruct((4, TILE, S)...  6.09 us
    pallas_call x1, Pallas kernels, update_two_rows(): pl.pallas_call(update_two_kernel, out_shape=jax.ShapeDtypeStruct((3, TILE...  5.31 us
    ppermute x4, starting transfers between devices, swapped(): return lax.ppermute(value, axis, pairs)  4.11 us
  transfers between devices with their start and end apart: 4, of which 0 were waited for; matrix products, arithmetic and copies ran while one was open for 2% of the time, Pallas kernels for 43%

profile of v4, /device:TPU:1, one launch (start us, length us, event | category | flops | bytes accessed | tf_op | source)
XLA Modules:
  0.0 202.4 jit_solution(9634066887317740472)
XLA Ops:
  0.6 3.3 %collective-permute-start = (bf16[4,256,512]{2,1,0:T(8,128)(2,1)}, bf16[4,256,512]{2,1,0:T(8,128)(2,1)S(1)}, u32[]{:S(2)}, u32[]{:S(2)}) collective-permute-start(bf16[4,256,512]{2,1,0:T(8,128)(2,1)} %bitcast.14), channel_id=1, source_target_pairs={{0,4},{4,0},{8,12},{12,8},{16,20},{20,16},{24,28},{28,24},{32,36},... | collective-permute-start | bytes 3145736 | tf_op jit(solution)/shard_map/ppermute | solution.py:26
  4.0 0.1 collective-permute-start.1
  4.1 0.4 collective-permute-start.3
  4.5 1.5 copy.10.map_ref.one_ref
  5.9 6.1 %spread.1.near_ref = bf16[4,256,1024]{2,1,0:T(8,128)(2,1)} custom-call(s32[64,1,4,3]{3,2,1,0:T(4,128)} %copy.10.map_ref.one_ref, bf16[3,256,3072]{2,1,0:T(8,128)(2,1)} %bitcast.7), custom_call_target="tpu_custom_call" | custom-call | tf_op jit(solution)/shard_map/spread/pallas_call | solution.py:138
  12.0 0.0 copy-done.4
  12.0 0.9 copy.11.mask_ref
  12.9 0.0 copy-done.6
  12.9 0.7 copy.13.two_ref
  13.7 0.0 copy-done.5
  13.7 0.8 copy.14.mask_ref
  14.5 0.0 collective-permute-done.1
  14.5 0.0 copy-done.3
  14.5 0.2 maximum_select_fusion.own_ref
  14.7 0.0 copy-start.1
  14.7 0.3 collective-permute-start.2
  15.0 0.0 collective-permute-done.peer_ref
  15.0 0.0 copy-start.7
  15.0 1.0 copy-done.7
  16.0 80.0 %front_1.1 = (f32[4,256,512]{2,1,0:T(8,128)}, bf16[4,768,1024]{2,1,0:T(8,128)(2,1)}) custom-call(s32[32,1,12,4]{3,2,1,0:T(8,128)} %copy.11.mask_ref, bf16[4,256,1024]{2,1,0:T(8,128)(2,1)} %spread.1.near_ref, bf16[4,256,512]{2,1,0:T(8,128)(2,1)} %bitcast.15, bf16[4,256,512]{2,1,0:T(8,128)(2,1)} %copy-done.7), custom_call_target="tpu_custom_call" | custom-call | flops 49999998976 | bytes 20000000 | tf_op jit(solution)/shard_map/front_1/pallas_call | solution.py:529
  96.0 0.0 copy-done.1
  96.0 0.0 collective-permute-done.2.peer_ref
  96.0 0.0 copy-start.8
  96.1 0.0 collective-permute-done.3.peer_ref
  96.1 17.7 %update_1.1 = (bf16[4,256,1024]{2,1,0:T(8,128)(2,1)}, bf16[3,256,768]{2,1,0:T(8,128)(2,1)}, bf16[3,256,768]{2,1,0:T(8,128)(2,1)}) custom-call(s32[64,1,4,3]{3,2,1,0:T(4,128)} %copy.10.map_ref.one_ref, s32[32,1,4,3]{3,2,1,0:T(4,128)} %copy.13.two_ref, bf16[4,768,1024]{2,1,0:T(8,128)(2,1)} %get-tuple-element.17.panels_ref, bf16[3,256,3072]{2,1,0:T(8,128)(2,1)} %bitcast.8, ...), custom_call_target="tpu_custom_call" | custom-call | tf_op jit(solution)/shard_map/update_1/pallas_call | solution.py:643
  113.8 0.0 copy-done.8
  113.8 80.3 %front_2.1 = (f32[4,256,256]{2,1,0:T(8,128)}, bf16[768,1024]{1,0:T(8,128)(2,1)}, bf16[4,256,1024]{2,1,0:T(8,128)(2,1)}, bf16[3,256,768]{2,1,0:T(8,128)(2,1)}) custom-call(s32[16,1,12,4]{3,2,1,0:T(8,128)} %copy.14.mask_ref, bf16[4,256,1024]{2,1,0:T(8,128)(2,1)} %get-tuple-element.18.near_ref, bf16[4,256,512]{2,1,0:T(8,128)(2,1)} %copy-done.1, ...), custom_call_target="tpu_custom_call" | custom-call | flops 49999998976 | bytes 20000000 | tf_op jit(solution)/shard_map/front_2/pallas_call | solution.py:529
  194.2 0.0 copy-start
  194.2 5.3 %update_2.1 = bf16[3,256,768]{2,1,0:T(8,128)(2,1)} custom-call(bf16[768,1024]{1,0:T(8,128)(2,1)} %get-tuple-element.23.x_ref, bf16[4,256,1024]{2,1,0:T(8,128)(2,1)} %get-tuple-element.24.y_ref, bf16[3,256,768]{2,1,0:T(8,128)(2,1)} %get-tuple-element.25.near_ref, bf16[3,256,768]{2,1,0:T(8,128)(2,1)} %get-tuple-element.26.far_ref), custom_call_target="tpu_custom_call" | custom-call | tf_op jit(solution)/shard_map/update_2/pallas_call | solution.py:677
  199.5 1.3 copy.17
  200.8 0.6 copy-done.2
  201.4 1.0 copy.18
  (6 shorter events, 0.0 us)
Async XLA Ops:
  0.6 14.4 %collective-permute-start = (bf16[4,256,512]{2,1,0:T(8,128)(2,1)}, bf16[4,256,512]{2,1,0:T(8,128)(2,1)S(1)}, u32[]{:S(2)}, u32[]{:S(2)}) collective-permute-start(bf16[4,256,512]{2,1,0:T(8,128)(2,1)} %bitcast.14), channel_id=1, source_target_pairs={{0,4},{4,0},{8,12},{12,8},{16,20},{20,16},{24,28},{28,24},{32,36},... | collective-permute-start | bytes 3145736 | tf_op jit(solution)/shard_map/ppermute | solution.py:26
  4.0 10.5 %collective-permute-start.1 = (bf16[4,256,256]{2,1,0:T(8,128)(2,1)}, bf16[4,256,256]{2,1,0:T(8,128)(2,1)S(1)}, u32[]{:S(2)}, u32[]{:S(2)}) collective-permute-start(bf16[4,256,256]{2,1,0:T(8,128)(2,1)} %bitcast.12), channel_id=1, source_target_pairs={{0,4},{4,0},{8,12},{12,8},{16,20},{20,16},{24,28},{28,24},{32,36},... | collective-permute-start | bytes 1572872 | tf_op jit(solution)/shard_map/ppermute | solution.py:26
  4.1 92.0 %collective-permute-start.3 = (bf16[3,256,3072]{2,1,0:T(8,128)(2,1)}, bf16[3,256,3072]{2,1,0:T(8,128)(2,1)}, u32[]{:S(2)}, u32[]{:S(2)}) collective-permute-start(bf16[3,256,3072]{2,1,0:T(8,128)(2,1)} %bitcast.6), channel_id=1, source_target_pairs={{0,4},{4,0},{8,12},{12,8},{16,20},{20,16},{24,28},{28,24},{32,36},... | collective-permute-start | bytes 14155784 | tf_op jit(solution)/shard_map/ppermute | solution.py:26
  5.9 6.1 %copy-start.4 = (s32[32,1,12,4]{0,3,2,1:T(4,128)S(1)}, s32[32,1,12,4]{0,3,2,1:T(4,128)}, u32[]{:S(2)}) copy-start(s32[32,1,12,4]{0,3,2,1:T(4,128)} %param.12) | copy-start | bytes 18436
  5.9 7.0 %copy-start.6 = (s32[32,1,4,3]{0,2,3,1:T(4,128)S(1)}, s32[32,1,4,3]{0,2,3,1:T(4,128)}, u32[]{:S(2)}) copy-start(s32[32,1,4,3]{0,2,3,1:T(4,128)} %param.11) | copy-start | bytes 4612
  5.9 7.7 %copy-start.5 = (s32[16,1,12,4]{0,3,2,1:T(4,128)S(1)}, s32[16,1,12,4]{0,3,2,1:T(4,128)}, u32[]{:S(2)}) copy-start(s32[16,1,12,4]{0,3,2,1:T(4,128)} %param.13) | copy-start | bytes 9220
  5.9 8.5 %copy-start.3 = (bf16[1,1,1,4,256,256]{5,4,3,2,1,0:T(8,128)(2,1)S(1)}, bf16[1,1,1,4,256,256]{5,4,3,2,1,0:T(8,128)(2,1)}, u32[]{:S(2)}) copy-start(bf16[1,1,1,4,256,256]{5,4,3,2,1,0:T(8,128)(2,1)} %param.9) | copy-start | bytes 1572868
  14.7 81.3 %copy-start.1 = (bf16[4,256,512]{2,1,0:T(8,128)(2,1)}, bf16[4,256,512]{2,1,0:T(8,128)(2,1)S(1)}, u32[]{:S(2)}) copy-start(bf16[4,256,512]{2,1,0:T(8,128)(2,1)S(1)} %maximum_select_fusion.own_ref) | copy-start | bytes 3145732
  14.7 81.3 %collective-permute-start.2 = (bf16[4,256,512]{2,1,0:T(8,128)(2,1)S(1)}, bf16[4,256,512]{2,1,0:T(8,128)(2,1)S(1)}, u32[]{:S(2)}, u32[]{:S(2)}) collective-permute-start(bf16[4,256,512]{2,1,0:T(8,128)(2,1)S(1)} %maximum_select_fusion.own_ref), channel_id=1, source_target_pairs={{0,8},{4,12},{8,0},{12,4},{16,24},{20,28},{24,16},{28,20},{32,40},... | collective-permute-start | bytes 3145736 | tf_op jit(solution)/shard_map/ppermute | solution.py:26
  15.0 1.0 copy-start.7
  96.0 17.8 %copy-start.8 = (bf16[4,256,512]{2,1,0:T(8,128)(2,1)}, bf16[4,256,512]{2,1,0:T(8,128)(2,1)S(1)}, u32[]{:S(2)}) copy-start(bf16[4,256,512]{2,1,0:T(8,128)(2,1)S(1)} %collective-permute-done.2.peer_ref) | copy-start | bytes 3145732
  194.2 5.3 %copy-start = (f32[4,256,512]{2,1,0:T(8,128)S(1)}, f32[4,256,512]{2,1,0:T(8,128)}, u32[]{:S(2)}) copy-start(f32[4,256,512]{2,1,0:T(8,128)} %get-tuple-element.15) | copy-start | bytes 6291460
  199.5 2.0 copy-start.2

commit v5 on v4

--- a/solution.py
+++ b/solution.py
@@ -46,9 +46,9 @@
 
 
 def source_of(map_ref, child, group, slot):
-    first = map_ref[child, 0, group, 0] == slot
-    second = map_ref[child, 0, group, 1] == slot
-    third = map_ref[child, 0, group, 2] == slot
+    first = map_ref[0, group, child] == slot
+    second = map_ref[1, group, child] == slot
+    third = map_ref[2, group, child] == slot
     index = jnp.where(first, 0, jnp.where(second, 1, 2))
     live = jnp.logical_or(first, jnp.logical_or(second, third))
     return index, live
@@ -112,8 +112,11 @@
     return lax.axis_index("leaf"), lax.axis_index("front")
 
 
-def spread_kernel(map_ref, child_ref, out_ref, sems):
+def spread_kernel(maps_ref, child_ref, out_ref, map_ref, map_sem, sems):
     leaf, group = place()
+    fetch = pltpu.make_async_copy(maps_ref, map_ref, map_sem)
+    fetch.start()
+    fetch.wait()
     copies = []
     for m in range(4):
         row, row_live = source_of(map_ref, leaf, group, m)
@@ -138,8 +141,12 @@
     return pl.pallas_call(
         spread_kernel,
         out_shape=jax.ShapeDtypeStruct((4, TILE, S), BF16),
-        in_specs=[pl.BlockSpec(memory_space=pltpu.SMEM), pl.BlockSpec(memory_space=pl.ANY)],
-        scratch_shapes=[pltpu.SemaphoreType.DMA((4, ST))],
+        in_specs=[pl.BlockSpec(memory_space=pl.ANY)] * 2,
+        scratch_shapes=[
+            pltpu.SMEM(tile_map.shape, jnp.int32),
+            pltpu.SemaphoreType.DMA,
+            pltpu.SemaphoreType.DMA((4, ST)),
+        ],
         name="spread",
     )(tile_map, child)
 
@@ -253,7 +260,7 @@
         factor_ref, panels_ref, *refs = refs
     else:
         given_ref, factor_ref, panel_ref, panels_ref, taken_ref, given_buf, given_sems, *refs = refs
-    (a_ref, high_ref, low_ref, inv_ref, near_top, init_top, far_top, near_rest, init_rest, far_rest,
+    (keep_ref, a_ref, high_ref, low_ref, inv_ref, near_top, init_top, far_top, near_rest, init_rest, far_rest,
      local_sems, top_sems, rest_sems, pivot_sems, panel_sems) = refs
     leaf, me = place()
     core = lax.rem(leaf, 2)
@@ -277,6 +284,7 @@
         pltpu.make_async_copy(own_ref.at[pl.ds(1, 3)], init_rest.at[bit], local_sems.at[4]),
         pltpu.make_async_copy(peer_ref.at[pl.ds(1, 3)], init_rest.at[1 - bit], local_sems.at[5]),
     ]
+    loads.append(pltpu.make_async_copy(mask_ref, keep_ref, local_sems.at[7]))
     if level == 2:
         loads.append(pltpu.make_async_copy(given_ref, given_buf, local_sems.at[6]))
     for load in loads:
@@ -381,7 +389,7 @@
             rest_copy(c, 0).wait_recv()
         for m in range(3):
             rows = slice(S + m * TILE, S + (m + 1) * TILE)
-            keep = mask_ref[leaf // (2 * level), 0, 4 * m + me, c].astype(F32)
+            keep = keep_ref[4 * m + me, c, leaf // (2 * level)].astype(F32)
             a_ref[rows, tile(c)] = (
                 near_rest[m, :, tile(c)].astype(F32)
                 + far_rest[m, :, tile(c)].astype(F32)
@@ -474,10 +482,6 @@
         def _():
             panels.forward(c - 1)
 
-        @pl.when(jnp.logical_and(odd, g > 1))
-        def _():
-            panels.finish(c - 1)
-
         @pl.when(odd)
         def _():
             if level == 1:
@@ -490,10 +494,13 @@
                 panels_ref[me, :, tile(c)] = high_ref[rows, tile(c)]
             panels.begin(c)
 
+        @pl.when(jnp.logical_and(odd, g > 1))
+        def _():
+            panels.finish(c - 1)
+
         return 0
 
     lax.fori_loop(0, S // G, step, 0)
-    panels.forward(ST - 1)
     width = S // (2 * level)
     start = lax.rem(leaf, 2 * level) * width
     part = pl.ds(pl.multiple_of(start, width), width)
@@ -502,6 +509,7 @@
     factor_ref[0] = jnp.where(row >= col, a_ref[tile(me), part], 0.0)
     for m in range(1, 4):
         factor_ref[m] = a_ref[S + (m - 1) * TILE : S + m * TILE, part]
+    panels.forward(ST - 1)
     panels.finish(ST - 1)
     for c in range(ST):
         panels.settle(c)
@@ -529,10 +537,11 @@
     return pl.pallas_call(
         functools.partial(front_kernel, level),
         out_shape=outs,
-        in_specs=[pl.BlockSpec(memory_space=pltpu.SMEM)] + [hbm] * (3 + len(given)),
+        in_specs=[hbm] * (4 + len(given)),
         out_specs=[vmem] * len(outs),
         scratch_shapes=[
             *([pltpu.VMEM((3, TILE, C), BF16), pltpu.SemaphoreType.DMA((2,))] if given else []),
+            pltpu.SMEM(tile_mask.shape, jnp.int32),
             pltpu.VMEM((S + C, S), F32),
             pltpu.VMEM((S + C, S), BF16),
             pltpu.VMEM((S + C, S), BF16),
@@ -543,7 +552,7 @@
             pltpu.VMEM((3, TILE, S), BF16),
             pltpu.VMEM((2, 3, TILE, S // 2), BF16),
             pltpu.VMEM((3, TILE, S), BF16),
-            pltpu.SemaphoreType.DMA((7,)),
+            pltpu.SemaphoreType.DMA((8,)),
             pltpu.SemaphoreType.DMA((2, ST)),
             pltpu.SemaphoreType.DMA((2, ST, 2)),
             pltpu.SemaphoreType.DMA((2, ST, 10)),
@@ -559,16 +568,27 @@
     )(tile_mask, near, own, peer, *given)
 
 
-def update_one_kernel(one_ref, two_ref, panels_ref, own_ref, peer_ref, pivot_out, near_out, far_out,
-                      x_buf, y_buf, tiles, total_ref, sems, x_sem):
+def update_one_kernel(ones_ref, twos_ref, panels_ref, own_ref, peer_ref, pivot_out, near_out, far_out,
+                      one_ref, two_ref, x_buf, y_buf, tiles, total_ref, sems, x_sem, map_sems):
     leaf, group = place()
     quarter = leaf % 4
     across = (quarter + 2) % 4
     sides = (own_ref, peer_ref)
+    x_copy = pltpu.make_async_copy(panels_ref.at[group], x_buf, x_sem)
+    x_copy.start()
+    pair = leaf // 2
+    fetches = [
+        pltpu.make_async_copy(ones_ref, one_ref, map_sems.at[0]),
+        pltpu.make_async_copy(twos_ref, two_ref, map_sems.at[1]),
+    ]
+    for fetch in fetches:
+        fetch.start()
+    for fetch in fetches:
+        fetch.wait()
 
     def column(i):
         t = jnp.where(i < 4, i, jnp.where(i < 7, 3 * quarter + i, 3 * across + i - 3))
-        tile, live = source_of(two_ref, leaf // 2, t % 4, t // 4)
+        tile, live = source_of(two_ref, pair, t % 4, t // 4)
         return t % 4, tile, live
 
     def there(i):
@@ -578,9 +598,7 @@
         return pltpu.make_async_copy(source, target, sems.at[i, k])
 
     rows = [[source_of(one_ref, leaf ^ side, group, 1 + s) for s in range(3)] for side in (0, 1)]
-    targets = [source_of(two_ref, leaf // 2, group, m) for m in range(4)]
-    x_copy = pltpu.make_async_copy(panels_ref.at[group], x_buf, x_sem)
-    x_copy.start()
+    targets = [source_of(two_ref, pair, group, m) for m in range(4)]
 
     def start(i, _):
         other, tile, _ = column(i)
@@ -613,24 +631,31 @@
                 total = total + jnp.where(live, slot[...].astype(F32), 0.0)
             total_ref[s] = total.astype(BF16)
 
-        def target(m):
+        def target(m, out, to, at):
             live = jnp.logical_and(targets[m][1], col_live)
-            return jnp.where(live, total_ref[targets[m][0]].astype(F32), 0.0).astype(BF16)
+
+            @pl.when(live)
+            def _():
+                out[to, :, there(at)] = total_ref[targets[m][0]]
+
+            @pl.when(jnp.logical_not(live))
+            def _():
+                out[to, :, there(at)] = jnp.zeros((TILE, TILE), BF16)
 
         @pl.when(i < 4)
         def _():
             for m in range(4):
-                pivot_out[m, :, there(i)] = target(m)
+                target(m, pivot_out, m, i)
 
         @pl.when(jnp.logical_and(i >= 4, i < 7))
         def _():
             for m in range(1, 4):
-                near_out[m - 1, :, there(i - 4)] = target(m)
+                target(m, near_out, m - 1, i - 4)
 
         @pl.when(i >= 7)
         def _():
             for m in range(1, 4):
-                far_out[m - 1, :, there(i - 7)] = target(m)
+                target(m, far_out, m - 1, i - 7)
 
         return 0
 
@@ -638,7 +663,6 @@
 
 
 def update_one_rows(map_one, map_two, panels, own, peer):
-    smem = pl.BlockSpec(memory_space=pltpu.SMEM)
     hbm = pl.BlockSpec(memory_space=pl.ANY)
     return pl.pallas_call(
         update_one_kernel,
@@ -647,21 +671,33 @@
             jax.ShapeDtypeStruct((3, TILE, C), BF16),
             jax.ShapeDtypeStruct((3, TILE, C), BF16),
         ],
-        in_specs=[smem, smem, hbm, hbm, hbm],
+        in_specs=[hbm] * 5,
         scratch_shapes=[
+            pltpu.SMEM(map_one.shape, jnp.int32),
+            pltpu.SMEM(map_two.shape, jnp.int32),
             pltpu.VMEM((C, S), BF16),
             pltpu.VMEM((10, TILE, S), BF16),
             pltpu.VMEM((2, 3, TILE, 10 * TILE), BF16),
             pltpu.VMEM((3, TILE, TILE), BF16),
             pltpu.SemaphoreType.DMA((10, 7)),
             pltpu.SemaphoreType.DMA,
+            pltpu.SemaphoreType.DMA((2,)),
         ],
         compiler_params=pltpu.CompilerParams(vmem_limit_bytes=VMEM_LIMIT),
         name="update_1",
     )(map_one, map_two, panels, own, peer)
 
 
-def update_two_kernel(x_ref, y_ref, near_ref, far_ref, out_ref):
+def update_two_kernel(x_ref, y_ref, near_ref, far_ref, one_in, two_in, out_ref, one_out, two_out,
+                      one_buf, two_buf, sems):
+    copies = [
+        pltpu.make_async_copy(one_in, one_buf, sems.at[0]),
+        pltpu.make_async_copy(two_in, two_buf, sems.at[1]),
+        pltpu.make_async_copy(one_buf, one_out, sems.at[2]),
+        pltpu.make_async_copy(two_buf, two_out, sems.at[3]),
+    ]
+    for copy in copies[:2]:
+        copy.start()
     leaf, _ = place()
     quarter = lax.rem(leaf, 4)
     for i in range(3):
@@ -670,17 +706,34 @@
         for m in range(3):
             front = near_ref[m, :, there].astype(F32) + far_ref[m, :, there].astype(F32)
             out_ref[m, :, there] = (front - product[m * TILE : (m + 1) * TILE, :]).astype(BF16)
-
-
-def update_two_rows(panel, panels, near, far):
+        if i == 0:
+            for k in (0, 1):
+                copies[k].wait()
+                copies[k + 2].start()
+    for copy in copies[2:]:
+        copy.wait()
+
+
+def update_two_rows(panel, panels, near, far, factor_one, factor_two):
     vmem = pl.BlockSpec(memory_space=pltpu.VMEM)
+    hbm = pl.BlockSpec(memory_space=pl.ANY)
     return pl.pallas_call(
         update_two_kernel,
-        out_shape=jax.ShapeDtypeStruct((3, TILE, C), BF16),
-        in_specs=[vmem] * 4,
+        out_shape=[
+            jax.ShapeDtypeStruct((3, TILE, C), BF16),
+            jax.ShapeDtypeStruct(factor_one.shape, F32),
+            jax.ShapeDtypeStruct(factor_two.shape, F32),
+        ],
+        in_specs=[vmem] * 4 + [hbm] * 2,
+        out_specs=[vmem, hbm, hbm],
+        scratch_shapes=[
+            pltpu.VMEM(factor_one.shape, F32),
+            pltpu.VMEM(factor_two.shape, F32),
+            pltpu.SemaphoreType.DMA((4,)),
+        ],
         compiler_params=pltpu.CompilerParams(vmem_limit_bytes=VMEM_LIMIT),
         name="update_2",
-    )(panel, panels, near, far)
+    )(panel, panels, near, far, factor_one, factor_two)
 
 
 def join_halves(mine, other, position):
@@ -694,6 +747,8 @@
     own = child_update[0, 0, 0]
     entries = sep_one[0, 0, 0]
     quarter = sep_two[0, 0, 0]
+    map_one, map_two = map_one[:, 0].transpose(2, 1, 0), map_two[:, 0].transpose(2, 1, 0)
+    mask_one, mask_two = mask_one[:, 0].transpose(1, 2, 0), mask_two[:, 0].transpose(1, 2, 0)
     entries_peer, quarter_peer, peer = swapped((entries, quarter, own), "leaf", 0)
     near = spread(map_one, own)
     half = join_halves(quarter, quarter_peer, leaf % 2)
@@ -702,7 +757,9 @@
     panels, half, half_far = lax.optimization_barrier((panels, half, half_far))
     near, rest, given = update_one_rows(map_one, map_two, panels, own, peer)
     factor_two, panel, panels, taken = front(2, mask_two, near, half, half_far, given)
-    update_two = update_two_rows(panel, panels, rest, taken)
+    update_two, factor_one, factor_two = update_two_rows(
+        panel, panels, rest, taken, factor_one, factor_two
+    )
     return (factor_one[None, None, None], factor_two[None, None, None], update_two[None, None, None])
 
 

time: 203 us -> 185 us (0.911)
  Pallas kernels: 189 us -> 179 us
  local copies, waits for them, and re-layouts: 7.83 us -> 1.02 us
    unnamed x24 -> x8, local copies, waits for them, and re-layouts: 7.83 us -> 1.02 us
    pallas_call x2, Pallas kernels: 160 us -> 154 us  [front(): pl.pallas_call(functools.partial(front_kernel, level), out_shape=outs, in...]
    pallas_call x1, Pallas kernels: 17.7 us -> 14.3 us  [update_one_rows(): pl.pallas_call(update_one_kernel, out_shape=[jax.ShapeDtypeStruct((4, TIL...]
    pallas_call x1, Pallas kernels: 6.09 us -> 4.01 us  [spread(): pl.pallas_call(spread_kernel, out_shape=jax.ShapeDtypeStruct((4, TILE, S)...]
  transfers between devices with their start and end apart: 4 -> 4, of which waited for: 0 -> 0; matrix products, arithmetic and copies ran while one was open for 2% -> 0% of each run, Pallas kernels for 43% -> 43%
where the time goes in v5:
time: 185 us
  Pallas kernels  179 us (97%)
  starting transfers between devices  4.11 us (2%)
    pallas_call x2, Pallas kernels, front(): pl.pallas_call(functools.partial(front_kernel, level), out_shape=outs, in...  154 us
    pallas_call x1, Pallas kernels, update_one_rows(): pl.pallas_call(update_one_kernel, out_shape=[jax.ShapeDtypeStruct((4, TIL...  14.3 us
    pallas_call x1, Pallas kernels, update_two_rows(): pl.pallas_call(update_two_kernel, out_shape=[jax.ShapeDtypeStruct((3, TIL...  7.03 us
    ppermute x4, starting transfers between devices, swapped(): return lax.ppermute(value, axis, pairs)  4.11 us
    pallas_call x1, Pallas kernels, spread(): pl.pallas_call(spread_kernel, out_shape=jax.ShapeDtypeStruct((4, TILE, S)...  4.01 us
  transfers between devices with their start and end apart: 4, of which 0 were waited for; matrix products, arithmetic and copies ran while one was open for 0% of the time, Pallas kernels for 43%

profile of v5, /device:TPU:1, one launch (start us, length us, event | category | flops | bytes accessed | tf_op | source)
XLA Modules:
  0.0 185.3 jit_solution(13291099630859953274)
XLA Ops:
  0.6 3.3 %collective-permute-start = (bf16[4,256,512]{2,1,0:T(8,128)(2,1)}, bf16[4,256,512]{2,1,0:T(8,128)(2,1)S(1)}, u32[]{:S(2)}, u32[]{:S(2)}) collective-permute-start(bf16[4,256,512]{2,1,0:T(8,128)(2,1)} %bitcast.28), channel_id=1, source_target_pairs={{0,4},{4,0},{8,12},{12,8},{16,20},{20,16},{24,28},{28,24},{32,36},... | collective-permute-start | bytes 3145736 | tf_op jit(solution)/shard_map/ppermute | solution.py:26
  4.0 0.1 collective-permute-start.1
  4.1 0.4 collective-permute-start.3
  4.5 0.0 copy-start.1
  4.5 4.0 %spread.1.near_ref = bf16[4,256,1024]{2,1,0:T(8,128)(2,1)} custom-call(s32[3,4,64]{2,1,0:T(4,128)} %bitcast.23, bf16[3,256,3072]{2,1,0:T(8,128)(2,1)} %bitcast.19), custom_call_target="tpu_custom_call" | custom-call | tf_op jit(solution)/shard_map/spread/pallas_call | solution.py:141
  8.5 0.0 collective-permute-done.1
  8.5 0.0 copy-done.1
  8.5 0.2 maximum_select_fusion.own_ref
  8.8 0.0 copy-start
  8.8 0.3 collective-permute-start.2
  9.1 0.0 collective-permute-done.peer_ref
  9.1 0.0 copy-start.2
  9.1 1.0 copy-done.2
  10.1 75.1 %front_1.1 = (f32[4,256,512]{2,1,0:T(8,128)}, bf16[4,768,1024]{2,1,0:T(8,128)(2,1)}) custom-call(s32[12,4,32]{2,1,0:T(4,128)} %bitcast.31, bf16[4,256,1024]{2,1,0:T(8,128)(2,1)} %spread.1.near_ref, bf16[4,256,512]{2,1,0:T(8,128)(2,1)} %bitcast.29, bf16[4,256,512]{2,1,0:T(8,128)(2,1)} %copy-done.2), custom_call_target="tpu_custom_call" | custom-call | flops 49999998976 | bytes 20000000 | tf_op jit(solution)/shard_map/front_1/pallas_call | solution.py:537
  85.2 0.0 copy-done
  85.2 0.0 collective-permute-done.2.peer_ref
  85.2 0.0 copy-start.3
  85.2 0.0 collective-permute-done.3.peer_ref
  85.2 14.3 %update_1.1 = (bf16[4,256,1024]{2,1,0:T(8,128)(2,1)}, bf16[3,256,768]{2,1,0:T(8,128)(2,1)}, bf16[3,256,768]{2,1,0:T(8,128)(2,1)}) custom-call(s32[3,4,64]{2,1,0:T(4,128)} %bitcast.24, s32[3,4,32]{2,1,0:T(4,128)} %bitcast.25, bf16[4,768,1024]{2,1,0:T(8,128)(2,1)} %get-tuple-element.19.panels_ref, bf16[3,256,3072]{2,1,0:T(8,128)(2,1)} %bitcast.20, ...), custom_call_target="tpu_custom_call" | custom-call | tf_op jit(solution)/shard_map/update_1/pallas_call | solution.py:667
  99.5 0.0 copy-done.3
  99.5 78.6 %front_2.1 = (f32[4,256,256]{2,1,0:T(8,128)}, bf16[768,1024]{1,0:T(8,128)(2,1)}, bf16[4,256,1024]{2,1,0:T(8,128)(2,1)}, bf16[3,256,768]{2,1,0:T(8,128)(2,1)}) custom-call(s32[12,4,16]{2,1,0:T(4,128)} %bitcast.32, bf16[4,256,1024]{2,1,0:T(8,128)(2,1)} %get-tuple-element.20.near_ref, bf16[4,256,512]{2,1,0:T(8,128)(2,1)} %copy-done, ...), custom_call_target="tpu_custom_call" | custom-call | flops 49999998976 | bytes 20000000 | tf_op jit(solution)/shard_map/front_2/pallas_call | solution.py:537
  178.1 7.0 %update_2.1 = (bf16[3,256,768]{2,1,0:T(8,128)(2,1)}, f32[4,256,512]{2,1,0:T(8,128)}, f32[4,256,256]{2,1,0:T(8,128)}) custom-call(bf16[768,1024]{1,0:T(8,128)(2,1)} %get-tuple-element.24.x_ref, bf16[4,256,1024]{2,1,0:T(8,128)(2,1)} %get-tuple-element.25.y_ref, bf16[3,256,768]{2,1,0:T(8,128)(2,1)} %get-tuple-element.26.near_ref, ...), custom_call_target="tpu_custom_call" | custom-call | tf_op jit(solution)/shard_map/update_2/pallas_call | solution.py:720
Async XLA Ops:
  0.6 8.4 %collective-permute-start = (bf16[4,256,512]{2,1,0:T(8,128)(2,1)}, bf16[4,256,512]{2,1,0:T(8,128)(2,1)S(1)}, u32[]{:S(2)}, u32[]{:S(2)}) collective-permute-start(bf16[4,256,512]{2,1,0:T(8,128)(2,1)} %bitcast.28), channel_id=1, source_target_pairs={{0,4},{4,0},{8,12},{12,8},{16,20},{20,16},{24,28},{28,24},{32,36},... | collective-permute-start | bytes 3145736 | tf_op jit(solution)/shard_map/ppermute | solution.py:26
  4.0 4.5 %collective-permute-start.1 = (bf16[4,256,256]{2,1,0:T(8,128)(2,1)}, bf16[4,256,256]{2,1,0:T(8,128)(2,1)S(1)}, u32[]{:S(2)}, u32[]{:S(2)}) collective-permute-start(bf16[4,256,256]{2,1,0:T(8,128)(2,1)} %bitcast.21), channel_id=1, source_target_pairs={{0,4},{4,0},{8,12},{12,8},{16,20},{20,16},{24,28},{28,24},{32,36},... | collective-permute-start | bytes 1572872 | tf_op jit(solution)/shard_map/ppermute | solution.py:26
  4.1 81.1 %collective-permute-start.3 = (bf16[3,256,3072]{2,1,0:T(8,128)(2,1)}, bf16[3,256,3072]{2,1,0:T(8,128)(2,1)}, u32[]{:S(2)}, u32[]{:S(2)}) collective-permute-start(bf16[3,256,3072]{2,1,0:T(8,128)(2,1)} %bitcast.18), channel_id=1, source_target_pairs={{0,4},{4,0},{8,12},{12,8},{16,20},{20,16},{24,28},{28,24},{32,36},... | collective-permute-start | bytes 14155784 | tf_op jit(solution)/shard_map/ppermute | solution.py:26
  4.5 4.0 %copy-start.1 = (bf16[1,1,1,4,256,256]{5,4,3,2,1,0:T(8,128)(2,1)S(1)}, bf16[1,1,1,4,256,256]{5,4,3,2,1,0:T(8,128)(2,1)}, u32[]{:S(2)}) copy-start(bf16[1,1,1,4,256,256]{5,4,3,2,1,0:T(8,128)(2,1)} %param.9) | copy-start | bytes 1572868
  8.8 76.4 %copy-start = (bf16[4,256,512]{2,1,0:T(8,128)(2,1)}, bf16[4,256,512]{2,1,0:T(8,128)(2,1)S(1)}, u32[]{:S(2)}) copy-start(bf16[4,256,512]{2,1,0:T(8,128)(2,1)S(1)} %maximum_select_fusion.own_ref) | copy-start | bytes 3145732
  8.8 76.4 %collective-permute-start.2 = (bf16[4,256,512]{2,1,0:T(8,128)(2,1)S(1)}, bf16[4,256,512]{2,1,0:T(8,128)(2,1)S(1)}, u32[]{:S(2)}, u32[]{:S(2)}) collective-permute-start(bf16[4,256,512]{2,1,0:T(8,128)(2,1)S(1)} %maximum_select_fusion.own_ref), channel_id=1, source_target_pairs={{0,8},{4,12},{8,0},{12,4},{16,24},{20,28},{24,16},{28,20},{32,40},... | collective-permute-start | bytes 3145736 | tf_op jit(solution)/shard_map/ppermute | solution.py:26
  9.1 1.0 copy-start.2
  85.2 14.3 %copy-start.3 = (bf16[4,256,512]{2,1,0:T(8,128)(2,1)}, bf16[4,256,512]{2,1,0:T(8,128)(2,1)S(1)}, u32[]{:S(2)}) copy-start(bf16[4,256,512]{2,1,0:T(8,128)(2,1)S(1)} %collective-permute-done.2.peer_ref) | copy-start | bytes 3145732
